TPU v7x, 256 devices: a whole 4x4x8 slice. The times are simulated.
256 devices in a mesh: node: 32 (over z, x), feat: 8 (over y, core).
Axes of the slice: x: 4, y: 4, z: 8, core: 2. Of those that a mesh axis runs over, the one named last changes fastest.
Arguments:
- out_grad: bfloat16 [256, 262144], P('feat', 'node'), may hold values from -6 to 6
- pre_act: bfloat16 [256, 262144], P('feat', 'node'), may hold values from -6 to 6
- in_act: bfloat16 [256, 262144], P(None, ('node', 'feat')), may hold values from -6 to 6
- weight: bfloat16 [256, 256], replicated, may hold values from -0.375 to 0.375
- tiles: bfloat16 [2048, 24, 128, 128], P('node'), may hold values from -0.4375 to 0.4375
- indices: int32 [2048, 24], P('node'), may hold values from 0 to 2047, as said below
- counts: int32 [2048], P('node'), may hold values from 1 to 24, as said below
Outputs:
- in_grad: bfloat16 [256, 262144], P(None, ('node', 'feat'))
- weight_grad: float32 [256, 256], replicated
Inputs may be any that keep to these rules, and one draw needn't show every extreme that they name: `indices`: the 24 column blocks named by one row block are distinct; slots at or after the row block's count are ignored. Each node device has a cap between 2 and 24, and its row blocks' counts are at most that cap, except for one row block in the whole graph whose count is 24.
All inputs are finite; a program needn't handle non-finite values.
Results may differ from a plain program's by a relative error of at most 0.012.
Values may be sent and summed in bfloat16 or wider, within the bound.
No kernel may reach another device: no remote copies, remote signals or barrier semaphores. Data moves between devices by JAX's collectives and lax.ppermute only.
A program may use at most 192 MiB of HBM per device.

v0:
```python
import collections
import functools

import jax
import jax.numpy as jnp
from jax import lax
from jax.experimental import pallas as pl
from jax.experimental.pallas import tpu as pltpu
from jax.sharding import PartitionSpec as P


RING = (8, 4)
FEAT = (4, 2)
SPLIT = 38
GROUPS = [("gb", (1,), True), ("gc", (2,), False), ("gd", (3, 4), True)]
UPPER = 33

QUAD = 4
GROUP = 8
DEPTH = 4


def plan_kernel(counts, work, length):
    rows = counts.shape[0]

    def one_row(r, n):
        runs = (counts[r] + QUAD - 1) // QUAD

        def one_run(c, n):
            work[n] = r * 32 + c * QUAD
            return n + 1

        return lax.fori_loop(0, runs, one_run, n)

    n = lax.fori_loop(0, rows, one_row, 0)
    length[0] = n
    for j in range(GROUP):
        work[n + j] = rows * 32


def make_plan(counts, slots):
    rows = counts.shape[0]
    smem = pl.BlockSpec(memory_space=pltpu.SMEM)
    return pl.pallas_call(
        plan_kernel,
        out_shape=(
            jax.ShapeDtypeStruct((rows * slots // QUAD + GROUP,), jnp.int32),
            jax.ShapeDtypeStruct((1,), jnp.int32),
        ),
        in_specs=[smem],
        out_specs=(smem, smem),
        name="plan",
    )(counts)


def gather_kernel(
    runs, here, work, length, counts, indices, tiles, *rest
):
    pieces = rest[: len(runs)]
    keep, cross, flat, held, stream, total, held_sem, stream_sem = rest[len(runs) :]
    rows, blk = counts.shape[0], tiles.shape[1]
    slots = tiles.shape[0] // rows
    groups = (length[0] + GROUP - 1) // GROUP
    shard = held.shape[0] // (RING[0] * RING[1])
    for piece, inside in zip(pieces, runs):
        start = 0
        for n, dz, dx, at in inside:
            z = lax.rem(here[2] + dz % RING[0], RING[0])
            x = lax.rem(here[3] + dx % RING[1], RING[1])
            place = (z * RING[1] + x) * shard + at
            pltpu.make_async_copy(
                piece.at[pl.ds(start, n)], held.at[pl.ds(place, n)], held_sem
            ).start()
            start += n

    def fetch(group):
        slot = lax.rem(group, DEPTH)
        for j in range(GROUP):
            entry = work[group * GROUP + j]
            r = jnp.minimum(lax.shift_right_logical(entry, 5), rows - 1)
            k = entry & 31
            pltpu.make_async_copy(
                tiles.at[pl.ds(r * slots + k, QUAD)], stream.at[slot, pl.ds(j * QUAD, QUAD)], stream_sem.at[slot]
            ).start()

    for g in range(DEPTH - 1):
        @pl.when(g < groups)
        def _():
            fetch(g)

    total[...] = jnp.zeros_like(total)
    pltpu.make_async_copy(held, held, held_sem).wait()

    def one_group(group, carry):
        @pl.when(group + DEPTH - 1 < groups)
        def _():
            fetch(group + DEPTH - 1)

        slot = lax.rem(group, DEPTH)
        pltpu.make_async_copy(
            tiles.at[pl.ds(0, GROUP * QUAD)], stream.at[slot], stream_sem.at[slot]
        ).wait()
        terms, where = [], []
        for j in range(GROUP):
            entry = work[group * GROUP + j]
            r = lax.shift_right_logical(entry, 5)
            k = entry & 31
            row = jnp.minimum(r, rows - 1)
            live = jnp.where(r < rows, counts[row], 0)
            picked = []
            for q in range(QUAD):
                block = held[indices[row * slots + k + q]]
                picked.append(jnp.where(k + q < live, block, jnp.zeros_like(block)))
            picked = jnp.concatenate(picked, axis=1)
            weights = jnp.concatenate([stream[slot, j * QUAD + q] for q in range(QUAD)], axis=1)
            terms.append(
                lax.dot_general(
                    picked, weights, (((1,), (1,)), ((), ())), preferred_element_type=jnp.float32
                )
            )
            where.append(r)
        for j in range(GROUP):
            total[where[j]] += terms[j]
        return carry

    lax.fori_loop(0, groups, one_group, 0)

    nodes = keep.shape[2]
    per_part = nodes // blk

    def one_step(s, carry):
        for c, out in enumerate((keep, cross)):
            part = lax.rem(here[0] + s, FEAT[0]) * FEAT[1] + lax.rem(here[1] + c, FEAT[1])
            for i in range(per_part):
                value = total[part * per_part + i].astype(jnp.bfloat16)
                out[s, :, i * blk : (i + 1) * blk] = value
                at = pl.multiple_of((s * FEAT[1] + c) * nodes + i * blk, blk)
                flat[:, pl.ds(at, blk)] = value
        return carry

    lax.fori_loop(0, FEAT[0], one_step, 0)


def gathered_sum(here, counts, indices, tiles, pieces, parts):
    rows, slots, blk, _ = tiles.shape
    feats = pieces[0].blocks.shape[1]
    total_blocks = sum(p.blocks.shape[0] for p in pieces)
    smem = pl.BlockSpec(memory_space=pltpu.SMEM)
    vmem = pl.BlockSpec(memory_space=pltpu.VMEM)
    anywhere = pl.BlockSpec(memory_space=pl.ANY)
    out_shape = (
        jax.ShapeDtypeStruct((FEAT[0], feats, rows * blk // parts), jnp.bfloat16),
        jax.ShapeDtypeStruct((FEAT[0], feats, rows * blk // parts), jnp.bfloat16),
        jax.ShapeDtypeStruct((feats, rows * blk), jnp.bfloat16),
    )
    work, length = make_plan(counts, slots)
    work_done = rows * slots // 2
    return pl.pallas_call(
        functools.partial(gather_kernel, [p.runs for p in pieces]),
        out_shape=out_shape,
        in_specs=[smem] * 5 + [anywhere] * (1 + len(pieces)),
        out_specs=(vmem, vmem, vmem),
        scratch_shapes=[
            pltpu.VMEM((total_blocks, feats, blk), pieces[0].blocks.dtype),
            pltpu.VMEM((DEPTH, GROUP * QUAD, blk, blk), tiles.dtype),
            pltpu.VMEM((rows + 1, feats, blk), jnp.float32),
            pltpu.SemaphoreType.DMA,
            pltpu.SemaphoreType.DMA((DEPTH,)),
        ],
        compiler_params=pltpu.CompilerParams(vmem_limit_bytes=48 * 1024 * 1024),
        cost_estimate=pl.CostEstimate(
            flops=2 * work_done * feats * blk * blk,
            bytes_accessed=2 * work_done * blk * blk + 2 * total_blocks * feats * blk,
            transcendentals=0,
        ),
        name="gathered_sum",
    )(
        here,
        work,
        length,
        counts,
        indices.reshape(-1),
        tiles.reshape(rows * slots, blk, blk),
        *(p.blocks for p in pieces),
    )


Piece = collections.namedtuple("Piece", "blocks runs")


def hop(piece, dz, dx):
    nz, nx = RING
    pairs = [
        (z * nx + x, (z + dz) % nz * nx + (x + dx) % nx) for z in range(nz) for x in range(nx)
    ]
    blocks = lax.ppermute(piece.blocks, "node", pairs)
    return Piece(blocks, [(n, z - dz, x - dx, at) for n, z, x, at in piece.runs])


def cut(piece, low, high):
    runs, seen = [], 0
    for n, z, x, at in piece.runs:
        first, last = max(low, seen), min(high, seen + n)
        if first < last:
            runs.append((last - first, z, x, at + first - seen))
        seen += n
    return Piece(piece.blocks[low:high], runs)


def join(*pieces):
    return Piece(
        jnp.concatenate([p.blocks for p in pieces], axis=0), [r for p in pieces for r in p.runs]
    )


def along(axis, piece, steps, upper):
    dz, dx = (1, 0) if axis == "z" else (0, 1)
    up = down = piece
    size = piece.blocks.shape[0]
    out = []
    for s in range(1, steps + 1):
        if s == steps and upper < size:
            down = cut(down, upper, size) if upper else down
            up = cut(up, 0, upper) if upper else None
        elif s == steps:
            down = None
        step = []
        if up is not None:
            up = hop(up, dz, dx)
            step.append(up)
        if down is not None:
            down = hop(down, -dz, -dx)
            step.append(down)
        out.append(step)
    return out


def gathered(own):
    shard = own.shape[0]
    a = Piece(own[:SPLIT], [(SPLIT, 0, 0, 0)])
    b = Piece(own[SPLIT:], [(shard - SPLIT, 0, 0, SPLIT)])
    az = along("z", a, RING[0] // 2, SPLIT)
    bx = along("x", b, RING[1] // 2, shard - SPLIT)
    across = join(b, *bx[0], *bx[1])
    pieces = [a, across]
    groups = [("ga", a, False)]
    for name, steps, one_way in GROUPS:
        joined = join(*(p for s in steps for p in az[s - 1]))
        groups.append((name, joined, one_way))
        pieces.append(joined)
    for name, piece, one_way in groups:
        for step in along("x", piece, RING[1] // 2, piece.blocks.shape[0] if one_way else 0):
            pieces += step
    for step in along("z", across, RING[0] // 2, UPPER):
        pieces += step
    return pieces


def over_feat(value, steps, swap):
    ny, nc = FEAT
    pairs = [
        (y * nc + c, (y + steps) % ny * nc + (c + swap) % nc) for y in range(ny) for c in range(nc)
    ]
    return lax.ppermute(value, "feat", pairs)


def column_kernel(scale, *refs):
    acts, flat, out, held, sems = refs[:-4], refs[-4], refs[-3], refs[-2], refs[-1]
    nodes = acts[0].shape[2]
    total = None
    loads = [
        pltpu.make_async_copy(pair, held.at[s], sems.at[s]) for s, pair in enumerate(acts)
    ]
    for load in loads:
        load.start()
    for s in range(len(acts) * acts[0].shape[0]):
        pair, c = s // acts[0].shape[0], s % acts[0].shape[0]
        if c == 0:
            loads[pair].wait()
        term = lax.dot_general(
            flat[:, s * nodes : (s + 1) * nodes],
            held[pair, c],
            (((1,), (1,)), ((), ())),
            preferred_element_type=jnp.float32,
        )
        total = term if total is None else total + term
    value = (total * scale).astype(jnp.bfloat16)
    for i in range(out.shape[0]):
        out[i] = value


def column_for_all(acts, flat, copies, scale):
    vmem = pl.BlockSpec(memory_space=pltpu.VMEM)
    features = acts[0].shape[1]
    return pl.pallas_call(
        functools.partial(column_kernel, scale),
        out_shape=jax.ShapeDtypeStruct((copies, flat.shape[0], features), jnp.bfloat16),
        in_specs=[pl.BlockSpec(memory_space=pl.ANY)] * len(acts) + [vmem],
        out_specs=vmem,
        scratch_shapes=[
            pltpu.VMEM((len(acts), *acts[0].shape), acts[0].dtype),
            pltpu.SemaphoreType.DMA((len(acts),)),
        ],
        compiler_params=pltpu.CompilerParams(vmem_limit_bytes=16 * 1024 * 1024),
        cost_estimate=pl.CostEstimate(
            flops=2 * features * flat.size, bytes_accessed=2 * features * flat.shape[1], transcendentals=0
        ),
        name="column",
    )(*acts, flat)


def sent_to_all(shard, axis):
    size = lax.axis_size(axis)
    return lax.all_to_all(
        jnp.broadcast_to(shard[None], (size, *shard.shape)), axis, 0, 0, tiled=True
    )


def per_device(out_grad, pre_act, in_act, weight, tiles, indices, counts):
    feats, local_nodes = out_grad.shape
    _, _, blk, _ = tiles.shape
    parts, nodes = lax.axis_size("feat"), lax.axis_size("node")
    assert nodes == RING[0] * RING[1] and parts == FEAT[0] * FEAT[1]
    grad_pre = jnp.where(pre_act > 0, out_grad, jnp.zeros_like(out_grad))
    own = grad_pre.reshape(feats, local_nodes // blk, blk).transpose(1, 0, 2)
    pieces = gathered(own)
    me = lax.axis_index("feat")
    spot = lax.axis_index("node")
    y, core = me // FEAT[1], me % FEAT[1]
    here = jnp.stack([y, core, spot // RING[1], spot % RING[1]]).astype(jnp.int32)
    both = jnp.stack([in_act, over_feat(in_act, 0, 1)])
    acts = [both] + [over_feat(both, -s, 0) for s in range(1, FEAT[0])]
    turned = jnp.concatenate(
        [
            lax.dynamic_slice_in_dim(
                weight,
                (lax.rem(y + FEAT[0] - s, FEAT[0]) * FEAT[1] + lax.rem(core + c, FEAT[1])) * feats,
                feats,
                1,
            )
            for s in range(FEAT[0])
            for c in range(FEAT[1])
        ],
        axis=1,
    )
    keep, cross, flat = gathered_sum(here, counts, indices, tiles, pieces, parts)

    scale = float(local_nodes * nodes) ** (-0.5)
    everyone = lax.all_to_all(
        column_for_all(acts, flat, nodes, scale), "node", 0, 0, tiled=True
    )
    column = jnp.sum(everyone.astype(jnp.float32), axis=0)
    columns = sent_to_all(column.astype(jnp.bfloat16), "feat")
    weight_grad = columns.reshape(-1, column.shape[1]).T.astype(jnp.float32)

    crossed = over_feat(cross, 0, 1)
    ready = [jnp.concatenate([keep[s], crossed[s]], axis=0) for s in range(FEAT[0])]
    received = [ready[0]] + [over_feat(ready[s], s, 0) for s in range(1, FEAT[0])]
    node_rows = jnp.concatenate(received, axis=0)
    in_grad = jnp.dot(turned, node_rows, preferred_element_type=jnp.float32).astype(jnp.bfloat16)
    return in_grad, weight_grad


def solution(mesh):
    in_specs = (
        P("feat", "node"),
        P("feat", "node"),
        P(None, ("node", "feat")),
        P(),
        P("node", None, None, None),
        P("node", None),
        P("node"),
    )
    out_specs = (P(None, ("node", "feat")), P())

    return jax.shard_map(
        per_device, mesh=mesh, in_specs=in_specs, out_specs=out_specs, check_vma=False
    )
```

profile of v0, /device:TPU:1, one launch (start us, length us, event | category | flops | bytes accessed | tf_op | source)
XLA Modules:
  0.0 207.0 jit_solution(11989369380890015137)
XLA Ops:
  0.6 1.4 bitcast_bitcast_fusion
  2.0 2.1 %collective-permute-start = (bf16[26,32,128]{2,1,0:T(8,128)(2,1)S(1)}, bf16[26,32,128]{2,1,0:T(8,128)(2,1)S(1)}, u32[]{:S(2)}, u32[]{:S(2)}) collective-permute-start(bf16[26,32,128]{2,1,0:T(8,128)(2,1)S(1)} %slice.49), channel_id=1, source_target_pairs={{0,8},{8,16},{16,24},{24,0},{32,40},{40,48},{48,56},{56,32},{64,72... | collective-permute-start | bytes 638984 | tf_op jit(solution)/shard_map/ppermute | solution.py:196
  4.2 1.7 collective-permute-start.3
  5.9 1.5 collective-permute-start.1
  7.3 1.3 collective-permute-done
  8.6 1.4 collective-permute-start.2
  10.0 5.8 %collective-permute-start.4 = (bf16[38,32,128]{2,1,0:T(8,128)(2,1)S(1)}, bf16[38,32,128]{2,1,0:T(8,128)(2,1)S(1)}, u32[]{:S(2)}, u32[]{:S(2)}) collective-permute-start(bf16[38,32,128]{2,1,0:T(8,128)(2,1)S(1)} %slice.48.rest_0_), channel_id=1, source_target_pairs={{0,224},{8,232},{16,240},{24,248},{32,0},{40,8},{48,16},{56,24},{6... | collective-permute-start | bytes 933896 | tf_op jit(solution)/shard_map/ppermute | solution.py:196
  15.9 2.1 %collective-permute-start.34 = (bf16[256,1024]{1,0:T(8,128)(2,1)}, bf16[256,1024]{1,0:T(8,128)(2,1)S(1)}, u32[]{:S(2)}, u32[]{:S(2)}) collective-permute-start(bf16[256,1024]{1,0:T(8,128)(2,1)} %param.9), channel_id=1, source_target_pairs={{0,1},{1,0},{2,3},{3,2},{4,5},{5,4},{6,7},{7,6},{8,9},{9,8},{10,11... | collective-permute-start | bytes 1572872 | tf_op jit(solution)/shard_map/ppermute | solution.py:264
  17.9 2.7 %collective-permute-start.11 = (bf16[38,32,128]{2,1,0:T(8,128)(2,1)S(1)}, bf16[38,32,128]{2,1,0:T(8,128)(2,1)S(1)}, u32[]{:S(2)}, u32[]{:S(2)}) collective-permute-start(bf16[38,32,128]{2,1,0:T(8,128)(2,1)S(1)} %slice.48.rest_0_), channel_id=1, source_target_pairs={{0,24},{8,0},{16,8},{24,16},{32,56},{40,32},{48,40},{56,48},{64,88... | collective-permute-start | bytes 933896 | tf_op jit(solution)/shard_map/ppermute | solution.py:196
  20.9 3.3 %collective-permute-start.23 = (bf16[104,32,128]{2,1,0:T(8,128)(2,1)S(1)}, bf16[104,32,128]{2,1,0:T(8,128)(2,1)S(1)}, u32[]{:S(2)}, u32[]{:S(2)}) collective-permute-start(bf16[104,32,128]{2,1,0:T(8,128)(2,1)S(1)} %pad_maximum_fusion.1.rest_1_), channel_id=1, source_target_pairs={{0,224},{8,232},{16,240},{24,248},{32,0},{40,8},{48,16},{56,24},{6... | collective-permute-start | bytes 2555912 | tf_op jit(solution)/shard_map/ppermute | solution.py:196
  24.2 3.2 %collective-permute-done.11.rest_6_ = bf16[38,32,128]{2,1,0:T(8,128)(2,1)S(1)} collective-permute-done((bf16[38,32,128]{2,1,0:T(8,128)(2,1)S(1)}, bf16[38,32,128]{2,1,0:T(8,128)(2,1)S(1)}, u32[]{:S(2)}, u32[]{:S(2)}) %collective-permute-start.11) | collective-permute-done | bytes 311328 | tf_op jit(solution)/shard_map/ppermute | solution.py:196
  28.1 2.4 %collective-permute-done.10.rest_5_ = bf16[38,32,128]{2,1,0:T(8,128)(2,1)S(1)} collective-permute-done((bf16[38,32,128]{2,1,0:T(8,128)(2,1)S(1)}, bf16[38,32,128]{2,1,0:T(8,128)(2,1)S(1)}, u32[]{:S(2)}, u32[]{:S(2)}) %collective-permute-start.10) | collective-permute-done | bytes 311328 | tf_op jit(solution)/shard_map/ppermute | solution.py:196
  30.5 1.0 collective-permute-start.12
  32.4 14.1 %collective-permute-done.6 = bf16[38,32,128]{2,1,0:T(8,128)(2,1)S(1)} collective-permute-done((bf16[38,32,128]{2,1,0:T(8,128)(2,1)S(1)}, bf16[38,32,128]{2,1,0:T(8,128)(2,1)S(1)}, u32[]{:S(2)}, u32[]{:S(2)}) %collective-permute-start.6) | collective-permute-done | bytes 311328 | tf_op jit(solution)/shard_map/ppermute | solution.py:196
  46.5 1.2 collective-permute-start.13
  48.4 1.5 collective-permute-start.14
  49.9 3.4 %collective-permute-start.8 = (bf16[38,32,128]{2,1,0:T(8,128)(2,1)S(1)}, bf16[38,32,128]{2,1,0:T(8,128)(2,1)S(1)}, u32[]{:S(2)}, u32[]{:S(2)}) collective-permute-start(bf16[38,32,128]{2,1,0:T(8,128)(2,1)S(1)} %collective-permute-done.6), channel_id=1, source_target_pairs={{0,224},{8,232},{16,240},{24,248},{32,0},{40,8},{48,16},{56,24},{6... | collective-permute-start | bytes 933896 | tf_op jit(solution)/shard_map/ppermute | solution.py:196
  53.4 3.8 %collective-permute-done.8 = bf16[38,32,128]{2,1,0:T(8,128)(2,1)S(1)} collective-permute-done((bf16[38,32,128]{2,1,0:T(8,128)(2,1)S(1)}, bf16[38,32,128]{2,1,0:T(8,128)(2,1)S(1)}, u32[]{:S(2)}, u32[]{:S(2)}) %collective-permute-start.8) | collective-permute-done | bytes 311328 | tf_op jit(solution)/shard_map/ppermute | solution.py:196
  57.2 1.5 collective-permute-start.17
  58.6 3.4 %collective-permute-start.25 = (bf16[104,32,128]{2,1,0:T(8,128)(2,1)S(1)}, bf16[104,32,128]{2,1,0:T(8,128)(2,1)S(1)}, u32[]{:S(2)}, u32[]{:S(2)}) collective-permute-start(bf16[104,32,128]{2,1,0:T(8,128)(2,1)S(1)} %collective-permute-done.23.rest_18_), channel_id=1, source_target_pairs={{0,224},{8,232},{16,240},{24,248},{32,0},{40,8},{48,16},{56,24},{6... | collective-permute-start | bytes 2555912 | tf_op jit(solution)/shard_map/ppermute | solution.py:196
  62.3 6.7 %collective-permute-done.9 = bf16[38,32,128]{2,1,0:T(8,128)(2,1)S(1)} collective-permute-done((bf16[38,32,128]{2,1,0:T(8,128)(2,1)S(1)}, bf16[38,32,128]{2,1,0:T(8,128)(2,1)S(1)}, u32[]{:S(2)}, u32[]{:S(2)}) %collective-permute-start.9) | collective-permute-done | bytes 311328 | tf_op jit(solution)/shard_map/ppermute | solution.py:196
  69.1 4.6 %collective-permute-done.17.rest_12_ = bf16[76,32,128]{2,1,0:T(8,128)(2,1)S(1)} collective-permute-done((bf16[76,32,128]{2,1,0:T(8,128)(2,1)S(1)}, bf16[76,32,128]{2,1,0:T(8,128)(2,1)S(1)}, u32[]{:S(2)}, u32[]{:S(2)}) %collective-permute-start.17) | collective-permute-done | bytes 622624 | tf_op jit(solution)/shard_map/ppermute | solution.py:196
  74.6 1.8 collective-permute-start.20
  76.4 3.4 %collective-permute-start.27 = (bf16[104,32,128]{2,1,0:T(8,128)(2,1)S(1)}, bf16[104,32,128]{2,1,0:T(8,128)(2,1)S(1)}, u32[]{:S(2)}, u32[]{:S(2)}) collective-permute-start(bf16[104,32,128]{2,1,0:T(8,128)(2,1)S(1)} %collective-permute-done.25.rest_20_), channel_id=1, source_target_pairs={{0,224},{8,232},{16,240},{24,248},{32,0},{40,8},{48,16},{56,24},{6... | collective-permute-start | bytes 2555912 | tf_op jit(solution)/shard_map/ppermute | solution.py:196
  79.8 6.0 %collective-permute-done.15.rest_10_ = bf16[76,32,128]{2,1,0:T(8,128)(2,1)S(1)} collective-permute-done((bf16[76,32,128]{2,1,0:T(8,128)(2,1)S(1)}, bf16[76,32,128]{2,1,0:T(8,128)(2,1)S(1)}, u32[]{:S(2)}, u32[]{:S(2)}) %collective-permute-start.15) | collective-permute-done | bytes 622624 | tf_op jit(solution)/shard_map/ppermute | solution.py:196
  86.6 19.1 %collective-permute-done.19.rest_14_ = bf16[114,32,128]{2,1,0:T(8,128)(2,1)S(1)} collective-permute-done((bf16[114,32,128]{2,1,0:T(8,128)(2,1)S(1)}, bf16[114,32,128]{2,1,0:T(8,128)(2,1)S(1)}, u32[]{:S(2)}, u32[]{:S(2)}) %collective-permute-start.19) | collective-permute-done | bytes 933920 | tf_op jit(solution)/shard_map/ppermute | solution.py:196
  105.7 1.5 pad_maximum_fusion.refs_0_
  107.2 2.8 %collective-permute-start.35 = (bf16[2,256,1024]{2,1,0:T(8,128)(2,1)S(1)}, bf16[2,256,1024]{2,1,0:T(8,128)(2,1)}, u32[]{:S(2)}, u32[]{:S(2)}) collective-permute-start(bf16[2,256,1024]{2,1,0:T(8,128)(2,1)S(1)} %pad_maximum_fusion.refs_0_), channel_id=1, source_target_pairs={{0,6},{1,7},{2,0},{3,1},{4,2},{5,3},{6,4},{7,5},{8,14},{9,15},{10,... | collective-permute-start | bytes 3145736 | tf_op jit(solution)/shard_map/ppermute | solution.py:264
  110.4 1.0 collective-permute-start.37
  112.2 1.4 collective-permute-start.29
  114.4 10.4 %collective-permute-done.21.rest_16_ = bf16[114,32,128]{2,1,0:T(8,128)(2,1)S(1)} collective-permute-done((bf16[114,32,128]{2,1,0:T(8,128)(2,1)S(1)}, bf16[114,32,128]{2,1,0:T(8,128)(2,1)S(1)}, u32[]{:S(2)}, u32[]{:S(2)}) %collective-permute-start.21) | collective-permute-done | bytes 933920 | tf_op jit(solution)/shard_map/ppermute | solution.py:196
  125.8 2.8 %plan.1 = (s32[392]{0:T(512)}, s32[1]{0:T(128)}) custom-call(s32[64]{0:T(128)} %counts.3), custom_call_target="tpu_custom_call" | custom-call | tf_op jit(solution)/shard_map/plan/pallas_call | solution.py:44
  128.6 1.4 copy.9
  130.9 2.1 %constant_dynamic-slice_fusion = (bf16[256,32]{1,0:T(8,128)(2,1)}, bf16[256,32]{1,0:T(8,128)(2,1)}, bf16[256,32]{1,0:T(8,128)(2,1)}, bf16[256,32]{1,0:T(8,128)(2...) fusion(bf16[256,256]{1,0:T(8,128)(2,1)} %param.10, ...), kind=kLoop, calls=%fused_computation.29 | loop fusion | bytes 262176 | tf_op jit(solution)/shard_map/dynamic_slice | solution.py:335
  133.0 1.9 concatenate.27
  134.9 1.1 copy-done.1
  136.0 1.0 copy-done.3
  137.0 1.0 copy-done.5
  139.3 12.3 %gathered_sum.1 = (bf16[4,32,1024]{2,1,0:T(8,128)(2,1)S(1)}, bf16[4,32,1024]{2,1,0:T(8,128)(2,1)S(1)}, bf16[32,8192]{1,0:T(8,128)(2,1)S(1)}) custom-call(s32[4]{0:T(128)S(1)} %pad_add_fusion.here, s32[392]{0:T(512)S(1)} %copy-done.7, s32[1]{0:T(128)} %get-tuple-element.8.length, s32[64]{0:T(128)S(1)} %copy-done.8, s32[1536]{0:T(1024)S(1)} %reshape.17.indices, ...), custom_call_target="tpu_custom_call" | custom-call | flops 805306368 | bytes 41943040 | tf_op jit(solution)/shard_map/gathered_sum/pallas_call | solution.py:158
  153.0 5.4 %collective-permute-done.37.refs_3_ = bf16[2,256,1024]{2,1,0:T(8,128)(2,1)} collective-permute-done((bf16[2,256,1024]{2,1,0:T(8,128)(2,1)S(1)}, bf16[2,256,1024]{2,1,0:T(8,128)(2,1)}, u32[]{:S(2)}, u32[]{:S(2)}) %collective-permute-start.37) | collective-permute-done | bytes 1048608 | tf_op jit(solution)/shard_map/ppermute | solution.py:264
  158.4 4.0 %column.1 = bf16[32,32,256]{2,1,0:T(8,128)(2,1)} custom-call(bf16[2,256,1024]{2,1,0:T(8,128)(2,1)S(1)} %pad_maximum_fusion.refs_0_, bf16[2,256,1024]{2,1,0:T(8,128)(2,1)} %collective-permute-done.35.refs_1_, bf16[2,256,1024]{2,1,0:T(8,128)(2,1)} %collective-permute-done.36.refs_2_, bf16[2,256,1024]{2,1,0:T(8,128)(2,1)} %collective-permute-done.37.refs_3_, ...), custom_call_target="tpu_custom_call" | custom-call | flops 134217728 | bytes 4194304 | tf_op jit(solution)/shard_map/column/pallas_call | solution.py:295
  162.5 8.3 %all-to-all-start = ((bf16[32,32,256]{2,1,0:T(8,128)(2,1)}), bf16[32,32,256]{2,1,0:T(8,128)(2,1)S(1)}, u32[]{:S(2)}, u32[]{:S(2)}) async-start(bf16[32,32,256]{2,1,0:T(8,128)(2,1)} %column.1), calls=%async_computation | async-start | bytes 1048576 | tf_op jit(solution)/shard_map/all_to_all | solution.py:349
  170.8 11.0 %collective-permute-start.30 = (bf16[4,32,1024]{2,1,0:T(8,128)(2,1)}, bf16[4,32,1024]{2,1,0:T(8,128)(2,1)S(1)}, u32[]{:S(2)}, u32[]{:S(2)}) collective-permute-start(bf16[4,32,1024]{2,1,0:T(8,128)(2,1)} %copy-done.9), channel_id=1, source_target_pairs={{0,1},{1,0},{2,3},{3,2},{4,5},{5,4},{6,7},{7,6},{8,9},{9,8},{10,11... | collective-permute-start | bytes 786440 | tf_op jit(solution)/shard_map/ppermute | solution.py:264
  183.6 2.8 %collective-permute-start.33 = (bf16[64,1024]{1,0:T(8,128)(2,1)S(1)}, bf16[64,1024]{1,0:T(8,128)(2,1)S(1)}, u32[]{:S(2)}, u32[]{:S(2)}) collective-permute-start(bf16[64,1024]{1,0:T(8,128)(2,1)S(1)} %pad_maximum_fusion.4), channel_id=1, source_target_pairs={{0,6},{1,7},{2,0},{3,1},{4,2},{5,3},{6,4},{7,5},{8,14},{9,15},{10,... | collective-permute-start | bytes 393224 | tf_op jit(solution)/shard_map/ppermute | solution.py:264
  187.7 8.6 %collective-permute-done.31 = bf16[64,1024]{1,0:T(8,128)(2,1)S(1)} collective-permute-done((bf16[64,1024]{1,0:T(8,128)(2,1)S(1)}, bf16[64,1024]{1,0:T(8,128)(2,1)S(1)}, u32[]{:S(2)}, u32[]{:S(2)}) %collective-permute-start.31) | collective-permute-done | bytes 131104 | tf_op jit(solution)/shard_map/ppermute | solution.py:264
  197.1 3.8 %all-to-all-start.1 = ((bf16[8,32,256]{2,1,0:T(8,128)(2,1)}), bf16[8,32,256]{2,1,0:T(8,128)(2,1)S(1)}, u32[]{:S(2)}, u32[]{:S(2)}) async-start(bf16[8,32,256]{2,1,0:T(8,128)(2,1)} %broadcast_in_dim.2), calls=%async_computation.1 | async-start | bytes 262144 | tf_op jit(solution)/shard_map/all_to_all | solution.py:314
  200.9 2.0 convolution_convert_fusion
  202.9 3.3 %all-to-all-done.1 = bf16[8,32,256]{2,1,0:T(8,128)(2,1)S(1)} async-done(((bf16[8,32,256]{2,1,0:T(8,128)(2,1)}), bf16[8,32,256]{2,1,0:T(8,128)(2,1)S(1)}, u32[]{:S(2)}, u32[]{:S(2)}) %all-to-all-start.1) | async-done | bytes 131104 | tf_op jit(solution)/shard_map/all_to_all | solution.py:314
  (117 shorter events, 15.9 us)
Async XLA Ops:
  2.0 6.6 %collective-permute-start = (bf16[26,32,128]{2,1,0:T(8,128)(2,1)S(1)}, bf16[26,32,128]{2,1,0:T(8,128)(2,1)S(1)}, u32[]{:S(2)}, u32[]{:S(2)}) collective-permute-start(bf16[26,32,128]{2,1,0:T(8,128)(2,1)S(1)} %slice.49), channel_id=1, source_target_pairs={{0,8},{8,16},{16,24},{24,0},{32,40},{40,48},{48,56},{56,32},{64,72... | collective-permute-start | bytes 638984 | tf_op jit(solution)/shard_map/ppermute | solution.py:196
  4.2 16.5 %collective-permute-start.3 = (bf16[38,32,128]{2,1,0:T(8,128)(2,1)S(1)}, bf16[38,32,128]{2,1,0:T(8,128)(2,1)S(1)}, u32[]{:S(2)}, u32[]{:S(2)}) collective-permute-start(bf16[38,32,128]{2,1,0:T(8,128)(2,1)S(1)} %slice.48.rest_0_), channel_id=1, source_target_pairs={{0,32},{8,40},{16,48},{24,56},{32,64},{40,72},{48,80},{56,88},{64,... | collective-permute-start | bytes 933896 | tf_op jit(solution)/shard_map/ppermute | solution.py:196
  5.9 12.1 %collective-permute-start.1 = (bf16[26,32,128]{2,1,0:T(8,128)(2,1)S(1)}, bf16[26,32,128]{2,1,0:T(8,128)(2,1)S(1)}, u32[]{:S(2)}, u32[]{:S(2)}) collective-permute-start(bf16[26,32,128]{2,1,0:T(8,128)(2,1)S(1)} %slice.49), channel_id=1, source_target_pairs={{0,24},{8,0},{16,8},{24,16},{32,56},{40,32},{48,40},{56,48},{64,88... | collective-permute-start | bytes 638984 | tf_op jit(solution)/shard_map/ppermute | solution.py:196
  8.6 12.0 %collective-permute-start.2 = (bf16[26,32,128]{2,1,0:T(8,128)(2,1)S(1)}, bf16[26,32,128]{2,1,0:T(8,128)(2,1)S(1)}, u32[]{:S(2)}, u32[]{:S(2)}) collective-permute-start(bf16[26,32,128]{2,1,0:T(8,128)(2,1)S(1)} %collective-permute-done), channel_id=1, source_target_pairs={{0,8},{8,16},{16,24},{24,0},{32,40},{40,48},{48,56},{56,32},{64,72... | collective-permute-start | bytes 638984 | tf_op jit(solution)/shard_map/ppermute | solution.py:196
  10.0 10.8 %collective-permute-start.4 = (bf16[38,32,128]{2,1,0:T(8,128)(2,1)S(1)}, bf16[38,32,128]{2,1,0:T(8,128)(2,1)S(1)}, u32[]{:S(2)}, u32[]{:S(2)}) collective-permute-start(bf16[38,32,128]{2,1,0:T(8,128)(2,1)S(1)} %slice.48.rest_0_), channel_id=1, source_target_pairs={{0,224},{8,232},{16,240},{24,248},{32,0},{40,8},{48,16},{56,24},{6... | collective-permute-start | bytes 933896 | tf_op jit(solution)/shard_map/ppermute | solution.py:196
  15.9 16.4 %collective-permute-start.34 = (bf16[256,1024]{1,0:T(8,128)(2,1)}, bf16[256,1024]{1,0:T(8,128)(2,1)S(1)}, u32[]{:S(2)}, u32[]{:S(2)}) collective-permute-start(bf16[256,1024]{1,0:T(8,128)(2,1)} %param.9), channel_id=1, source_target_pairs={{0,1},{1,0},{2,3},{3,2},{4,5},{5,4},{6,7},{7,6},{8,9},{9,8},{10,11... | collective-permute-start | bytes 1572872 | tf_op jit(solution)/shard_map/ppermute | solution.py:264
  17.9 9.4 %collective-permute-start.11 = (bf16[38,32,128]{2,1,0:T(8,128)(2,1)S(1)}, bf16[38,32,128]{2,1,0:T(8,128)(2,1)S(1)}, u32[]{:S(2)}, u32[]{:S(2)}) collective-permute-start(bf16[38,32,128]{2,1,0:T(8,128)(2,1)S(1)} %slice.48.rest_0_), channel_id=1, source_target_pairs={{0,24},{8,0},{16,8},{24,16},{32,56},{40,32},{48,40},{56,48},{64,88... | collective-permute-start | bytes 933896 | tf_op jit(solution)/shard_map/ppermute | solution.py:196
  20.6 9.8 %collective-permute-start.10 = (bf16[38,32,128]{2,1,0:T(8,128)(2,1)S(1)}, bf16[38,32,128]{2,1,0:T(8,128)(2,1)S(1)}, u32[]{:S(2)}, u32[]{:S(2)}) collective-permute-start(bf16[38,32,128]{2,1,0:T(8,128)(2,1)S(1)} %slice.48.rest_0_), channel_id=1, source_target_pairs={{0,8},{8,16},{16,24},{24,0},{32,40},{40,48},{48,56},{56,32},{64,72... | collective-permute-start | bytes 933896 | tf_op jit(solution)/shard_map/ppermute | solution.py:196
  20.6 10.8 %collective-permute-start.5 = (bf16[38,32,128]{2,1,0:T(8,128)(2,1)S(1)}, bf16[38,32,128]{2,1,0:T(8,128)(2,1)S(1)}, u32[]{:S(2)}, u32[]{:S(2)}) collective-permute-start(bf16[38,32,128]{2,1,0:T(8,128)(2,1)S(1)} %collective-permute-done.3), channel_id=1, source_target_pairs={{0,32},{8,40},{16,48},{24,56},{32,64},{40,72},{48,80},{56,88},{64,... | collective-permute-start | bytes 933896 | tf_op jit(solution)/shard_map/ppermute | solution.py:196
  20.8 89.5 %copy-start.10 = (bf16[104,32,128]{2,1,0:T(8,128)(2,1)}, bf16[104,32,128]{2,1,0:T(8,128)(2,1)S(1)}, u32[]{:S(2)}) copy-start(bf16[104,32,128]{2,1,0:T(8,128)(2,1)S(1)} %pad_maximum_fusion.1.rest_1_) | copy-start | bytes 2555908
  20.9 37.8 %collective-permute-start.23 = (bf16[104,32,128]{2,1,0:T(8,128)(2,1)S(1)}, bf16[104,32,128]{2,1,0:T(8,128)(2,1)S(1)}, u32[]{:S(2)}, u32[]{:S(2)}) collective-permute-start(bf16[104,32,128]{2,1,0:T(8,128)(2,1)S(1)} %pad_maximum_fusion.1.rest_1_), channel_id=1, source_target_pairs={{0,224},{8,232},{16,240},{24,248},{32,0},{40,8},{48,16},{56,24},{6... | collective-permute-start | bytes 2555912 | tf_op jit(solution)/shard_map/ppermute | solution.py:196
  27.3 19.1 %collective-permute-start.6 = (bf16[38,32,128]{2,1,0:T(8,128)(2,1)S(1)}, bf16[38,32,128]{2,1,0:T(8,128)(2,1)S(1)}, u32[]{:S(2)}, u32[]{:S(2)}) collective-permute-start(bf16[38,32,128]{2,1,0:T(8,128)(2,1)S(1)} %collective-permute-done.4), channel_id=1, source_target_pairs={{0,224},{8,232},{16,240},{24,248},{32,0},{40,8},{48,16},{56,24},{6... | collective-permute-start | bytes 933896 | tf_op jit(solution)/shard_map/ppermute | solution.py:196
  30.5 17.2 %collective-permute-start.12 = (bf16[38,32,128]{2,1,0:T(8,128)(2,1)S(1)}, bf16[38,32,128]{2,1,0:T(8,128)(2,1)S(1)}, u32[]{:S(2)}, u32[]{:S(2)}) collective-permute-start(bf16[38,32,128]{2,1,0:T(8,128)(2,1)S(1)} %collective-permute-done.11.rest_6_), channel_id=1, source_target_pairs={{0,24},{8,0},{16,8},{24,16},{32,56},{40,32},{48,40},{56,48},{64,88... | collective-permute-start | bytes 933896 | tf_op jit(solution)/shard_map/ppermute | solution.py:196
  31.5 18.4 %collective-permute-start.7 = (bf16[38,32,128]{2,1,0:T(8,128)(2,1)S(1)}, bf16[38,32,128]{2,1,0:T(8,128)(2,1)S(1)}, u32[]{:S(2)}, u32[]{:S(2)}) collective-permute-start(bf16[38,32,128]{2,1,0:T(8,128)(2,1)S(1)} %collective-permute-done.5), channel_id=1, source_target_pairs={{0,32},{8,40},{16,48},{24,56},{32,64},{40,72},{48,80},{56,88},{64,... | collective-permute-start | bytes 933896 | tf_op jit(solution)/shard_map/ppermute | solution.py:196
  32.3 29.9 %collective-permute-start.22 = (bf16[104,32,128]{2,1,0:T(8,128)(2,1)S(1)}, bf16[104,32,128]{2,1,0:T(8,128)(2,1)S(1)}, u32[]{:S(2)}, u32[]{:S(2)}) collective-permute-start(bf16[104,32,128]{2,1,0:T(8,128)(2,1)S(1)} %pad_maximum_fusion.1.rest_1_), channel_id=1, source_target_pairs={{0,32},{8,40},{16,48},{24,56},{32,64},{40,72},{48,80},{56,88},{64,... | collective-permute-start | bytes 2555912 | tf_op jit(solution)/shard_map/ppermute | solution.py:196
  46.5 15.6 %collective-permute-start.13 = (bf16[76,32,128]{2,1,0:T(8,128)(2,1)S(1)}, bf16[76,32,128]{2,1,0:T(8,128)(2,1)S(1)}, u32[]{:S(2)}, u32[]{:S(2)}) collective-permute-start(bf16[76,32,128]{2,1,0:T(8,128)(2,1)S(1)} %constant_dynamic-update-slice_fusion.rest_2_), channel_id=1, source_target_pairs={{0,8},{8,16},{16,24},{24,0},{32,40},{40,48},{48,56},{56,32},{64,72... | collective-permute-start | bytes 1867784 | tf_op jit(solution)/shard_map/ppermute | solution.py:196
  48.4 13.6 %collective-permute-start.14 = (bf16[76,32,128]{2,1,0:T(8,128)(2,1)S(1)}, bf16[76,32,128]{2,1,0:T(8,128)(2,1)S(1)}, u32[]{:S(2)}, u32[]{:S(2)}) collective-permute-start(bf16[76,32,128]{2,1,0:T(8,128)(2,1)S(1)} %constant_dynamic-update-slice_fusion.rest_2_), channel_id=1, source_target_pairs={{0,24},{8,0},{16,8},{24,16},{32,56},{40,32},{48,40},{56,48},{64,88... | collective-permute-start | bytes 1867784 | tf_op jit(solution)/shard_map/ppermute | solution.py:196
  49.9 7.3 %collective-permute-start.8 = (bf16[38,32,128]{2,1,0:T(8,128)(2,1)S(1)}, bf16[38,32,128]{2,1,0:T(8,128)(2,1)S(1)}, u32[]{:S(2)}, u32[]{:S(2)}) collective-permute-start(bf16[38,32,128]{2,1,0:T(8,128)(2,1)S(1)} %collective-permute-done.6), channel_id=1, source_target_pairs={{0,224},{8,232},{16,240},{24,248},{32,0},{40,8},{48,16},{56,24},{6... | collective-permute-start | bytes 933896 | tf_op jit(solution)/shard_map/ppermute | solution.py:196
  57.2 16.5 %collective-permute-start.17 = (bf16[76,32,128]{2,1,0:T(8,128)(2,1)S(1)}, bf16[76,32,128]{2,1,0:T(8,128)(2,1)S(1)}, u32[]{:S(2)}, u32[]{:S(2)}) collective-permute-start(bf16[76,32,128]{2,1,0:T(8,128)(2,1)S(1)} %constant_dynamic-update-slice_fusion.2.rest_3_), channel_id=1, source_target_pairs={{0,24},{8,0},{16,8},{24,16},{32,56},{40,32},{48,40},{56,48},{64,88... | collective-permute-start | bytes 1867784 | tf_op jit(solution)/shard_map/ppermute | solution.py:196
  58.6 27.2 %copy-start.17 = (bf16[104,32,128]{2,1,0:T(8,128)(2,1)}, bf16[104,32,128]{2,1,0:T(8,128)(2,1)S(1)}, u32[]{:S(2)}) copy-start(bf16[104,32,128]{2,1,0:T(8,128)(2,1)S(1)} %collective-permute-done.23.rest_18_) | copy-start | bytes 2555908
  58.6 17.7 %collective-permute-start.25 = (bf16[104,32,128]{2,1,0:T(8,128)(2,1)S(1)}, bf16[104,32,128]{2,1,0:T(8,128)(2,1)S(1)}, u32[]{:S(2)}, u32[]{:S(2)}) collective-permute-start(bf16[104,32,128]{2,1,0:T(8,128)(2,1)S(1)} %collective-permute-done.23.rest_18_), channel_id=1, source_target_pairs={{0,224},{8,232},{16,240},{24,248},{32,0},{40,8},{48,16},{56,24},{6... | collective-permute-start | bytes 2555912 | tf_op jit(solution)/shard_map/ppermute | solution.py:196
  62.0 7.0 %collective-permute-start.9 = (bf16[38,32,128]{2,1,0:T(8,128)(2,1)S(1)}, bf16[38,32,128]{2,1,0:T(8,128)(2,1)S(1)}, u32[]{:S(2)}, u32[]{:S(2)}) collective-permute-start(bf16[38,32,128]{2,1,0:T(8,128)(2,1)S(1)} %collective-permute-done.7), channel_id=1, source_target_pairs={{0,32},{8,40},{16,48},{24,56},{32,64},{40,72},{48,80},{56,88},{64,... | collective-permute-start | bytes 933896 | tf_op jit(solution)/shard_map/ppermute | solution.py:196
  62.0 43.6 %copy-start = (bf16[76,32,128]{2,1,0:T(8,128)(2,1)}, bf16[76,32,128]{2,1,0:T(8,128)(2,1)S(1)}, u32[]{:S(2)}) copy-start(bf16[76,32,128]{2,1,0:T(8,128)(2,1)S(1)} %collective-permute-done.14.rest_9_) | copy-start | bytes 1867780
  62.1 12.5 %collective-permute-start.16 = (bf16[76,32,128]{2,1,0:T(8,128)(2,1)S(1)}, bf16[76,32,128]{2,1,0:T(8,128)(2,1)}, u32[]{:S(2)}, u32[]{:S(2)}) collective-permute-start(bf16[76,32,128]{2,1,0:T(8,128)(2,1)S(1)} %constant_dynamic-update-slice_fusion.2.rest_3_), channel_id=1, source_target_pairs={{0,8},{8,16},{16,24},{24,0},{32,40},{40,48},{48,56},{56,32},{64,72... | collective-permute-start | bytes 1867784 | tf_op jit(solution)/shard_map/ppermute | solution.py:196
  62.2 43.5 %copy-start.18 = (bf16[104,32,128]{2,1,0:T(8,128)(2,1)}, bf16[104,32,128]{2,1,0:T(8,128)(2,1)S(1)}, u32[]{:S(2)}) copy-start(bf16[104,32,128]{2,1,0:T(8,128)(2,1)S(1)} %collective-permute-done.22.rest_17_) | copy-start | bytes 2555908
  62.2 23.6 %collective-permute-start.24 = (bf16[104,32,128]{2,1,0:T(8,128)(2,1)S(1)}, bf16[104,32,128]{2,1,0:T(8,128)(2,1)S(1)}, u32[]{:S(2)}, u32[]{:S(2)}) collective-permute-start(bf16[104,32,128]{2,1,0:T(8,128)(2,1)S(1)} %collective-permute-done.22.rest_17_), channel_id=1, source_target_pairs={{0,32},{8,40},{16,48},{24,56},{32,64},{40,72},{48,80},{56,88},{64,... | collective-permute-start | bytes 2555912 | tf_op jit(solution)/shard_map/ppermute | solution.py:196
  69.0 16.8 %collective-permute-start.15 = (bf16[76,32,128]{2,1,0:T(8,128)(2,1)S(1)}, bf16[76,32,128]{2,1,0:T(8,128)(2,1)S(1)}, u32[]{:S(2)}, u32[]{:S(2)}) collective-permute-start(bf16[76,32,128]{2,1,0:T(8,128)(2,1)S(1)} %collective-permute-done.13.rest_8_), channel_id=1, source_target_pairs={{0,8},{8,16},{16,24},{24,0},{32,40},{40,48},{48,56},{56,32},{64,72... | collective-permute-start | bytes 1867784 | tf_op jit(solution)/shard_map/ppermute | solution.py:196
  69.0 43.2 %copy-start.12 = (bf16[114,32,128]{2,1,0:T(8,128)(2,1)}, bf16[114,32,128]{2,1,0:T(8,128)(2,1)S(1)}, u32[]{:S(2)}) copy-start(bf16[114,32,128]{2,1,0:T(8,128)(2,1)S(1)} %constant_dynamic-update-slice_fusion.4.rest_4_) | copy-start | bytes 2801668
  73.7 51.7 %copy-start.21 = (bf16[76,32,128]{2,1,0:T(8,128)(2,1)}, bf16[76,32,128]{2,1,0:T(8,128)(2,1)S(1)}, u32[]{:S(2)}) copy-start(bf16[76,32,128]{2,1,0:T(8,128)(2,1)S(1)} %collective-permute-done.17.rest_12_) | copy-start | bytes 1867780
  73.7 32.0 %collective-permute-start.19 = (bf16[114,32,128]{2,1,0:T(8,128)(2,1)S(1)}, bf16[114,32,128]{2,1,0:T(8,128)(2,1)S(1)}, u32[]{:S(2)}, u32[]{:S(2)}) collective-permute-start(bf16[114,32,128]{2,1,0:T(8,128)(2,1)S(1)} %constant_dynamic-update-slice_fusion.4.rest_4_), channel_id=1, source_target_pairs={{0,8},{8,16},{16,24},{24,0},{32,40},{40,48},{48,56},{56,32},{64,72... | collective-permute-start | bytes 2801672 | tf_op jit(solution)/shard_map/ppermute | solution.py:196
  74.6 35.4 %collective-permute-start.20 = (bf16[114,32,128]{2,1,0:T(8,128)(2,1)S(1)}, bf16[114,32,128]{2,1,0:T(8,128)(2,1)S(1)}, u32[]{:S(2)}, u32[]{:S(2)}) collective-permute-start(bf16[114,32,128]{2,1,0:T(8,128)(2,1)S(1)} %constant_dynamic-update-slice_fusion.4.rest_4_), channel_id=1, source_target_pairs={{0,24},{8,0},{16,8},{24,16},{32,56},{40,32},{48,40},{56,48},{64,88... | collective-permute-start | bytes 2801672 | tf_op jit(solution)/shard_map/ppermute | solution.py:196
  76.4 49.0 %copy-start.19 = (bf16[104,32,128]{2,1,0:T(8,128)(2,1)}, bf16[104,32,128]{2,1,0:T(8,128)(2,1)S(1)}, u32[]{:S(2)}) copy-start(bf16[104,32,128]{2,1,0:T(8,128)(2,1)S(1)} %collective-permute-done.25.rest_20_) | copy-start | bytes 2555908
  76.4 34.0 %collective-permute-start.27 = (bf16[104,32,128]{2,1,0:T(8,128)(2,1)S(1)}, bf16[104,32,128]{2,1,0:T(8,128)(2,1)S(1)}, u32[]{:S(2)}, u32[]{:S(2)}) collective-permute-start(bf16[104,32,128]{2,1,0:T(8,128)(2,1)S(1)} %collective-permute-done.25.rest_20_), channel_id=1, source_target_pairs={{0,224},{8,232},{16,240},{24,248},{32,0},{40,8},{48,16},{56,24},{6... | collective-permute-start | bytes 2555912 | tf_op jit(solution)/shard_map/ppermute | solution.py:196
  85.8 21.4 %collective-permute-start.18 = (bf16[76,32,128]{2,1,0:T(8,128)(2,1)S(1)}, bf16[76,32,128]{2,1,0:T(8,128)(2,1)S(1)}, u32[]{:S(2)}, u32[]{:S(2)}) collective-permute-start(bf16[76,32,128]{2,1,0:T(8,128)(2,1)S(1)} %collective-permute-done.17.rest_12_), channel_id=1, source_target_pairs={{0,24},{8,0},{16,8},{24,16},{32,56},{40,32},{48,40},{56,48},{64,88... | collective-permute-start | bytes 1867784 | tf_op jit(solution)/shard_map/ppermute | solution.py:196
  85.8 39.6 %copy-start.20 = (bf16[104,32,128]{2,1,0:T(8,128)(2,1)}, bf16[104,32,128]{2,1,0:T(8,128)(2,1)S(1)}, u32[]{:S(2)}) copy-start(bf16[104,32,128]{2,1,0:T(8,128)(2,1)S(1)} %collective-permute-done.24.rest_19_) | copy-start | bytes 2555908
  85.8 26.4 %collective-permute-start.26 = (bf16[104,32,128]{2,1,0:T(8,128)(2,1)S(1)}, bf16[104,32,128]{2,1,0:T(8,128)(2,1)S(1)}, u32[]{:S(2)}, u32[]{:S(2)}) collective-permute-start(bf16[104,32,128]{2,1,0:T(8,128)(2,1)S(1)} %collective-permute-done.24.rest_19_), channel_id=1, source_target_pairs={{0,32},{8,40},{16,48},{24,56},{32,64},{40,72},{48,80},{56,88},{64,... | collective-permute-start | bytes 2555912 | tf_op jit(solution)/shard_map/ppermute | solution.py:196
  105.7 19.2 %collective-permute-start.21 = (bf16[114,32,128]{2,1,0:T(8,128)(2,1)S(1)}, bf16[114,32,128]{2,1,0:T(8,128)(2,1)S(1)}, u32[]{:S(2)}, u32[]{:S(2)}) collective-permute-start(bf16[114,32,128]{2,1,0:T(8,128)(2,1)S(1)} %collective-permute-done.19.rest_14_), channel_id=1, source_target_pairs={{0,8},{8,16},{16,24},{24,0},{32,40},{40,48},{48,56},{56,32},{64,72... | collective-permute-start | bytes 2801672 | tf_op jit(solution)/shard_map/ppermute | solution.py:196
  107.2 45.8 %collective-permute-start.35 = (bf16[2,256,1024]{2,1,0:T(8,128)(2,1)S(1)}, bf16[2,256,1024]{2,1,0:T(8,128)(2,1)}, u32[]{:S(2)}, u32[]{:S(2)}) collective-permute-start(bf16[2,256,1024]{2,1,0:T(8,128)(2,1)S(1)} %pad_maximum_fusion.refs_0_), channel_id=1, source_target_pairs={{0,6},{1,7},{2,0},{3,1},{4,2},{5,3},{6,4},{7,5},{8,14},{9,15},{10,... | collective-permute-start | bytes 3145736 | tf_op jit(solution)/shard_map/ppermute | solution.py:264
  110.0 43.0 %collective-permute-start.36 = (bf16[2,256,1024]{2,1,0:T(8,128)(2,1)S(1)}, bf16[2,256,1024]{2,1,0:T(8,128)(2,1)}, u32[]{:S(2)}, u32[]{:S(2)}) collective-permute-start(bf16[2,256,1024]{2,1,0:T(8,128)(2,1)S(1)} %pad_maximum_fusion.refs_0_), channel_id=1, source_target_pairs={{0,4},{1,5},{2,6},{3,7},{4,0},{5,1},{6,2},{7,3},{8,12},{9,13},{10,... | collective-permute-start | bytes 3145736 | tf_op jit(solution)/shard_map/ppermute | solution.py:264
  110.4 48.1 %collective-permute-start.37 = (bf16[2,256,1024]{2,1,0:T(8,128)(2,1)S(1)}, bf16[2,256,1024]{2,1,0:T(8,128)(2,1)}, u32[]{:S(2)}, u32[]{:S(2)}) collective-permute-start(bf16[2,256,1024]{2,1,0:T(8,128)(2,1)S(1)} %pad_maximum_fusion.refs_0_), channel_id=1, source_target_pairs={{0,2},{1,3},{2,4},{3,5},{4,6},{5,7},{6,0},{7,1},{8,10},{9,11},{10,... | collective-permute-start | bytes 3145736 | tf_op jit(solution)/shard_map/ppermute | solution.py:264
  112.2 22.7 %collective-permute-start.29 = (bf16[71,32,128]{2,1,0:T(8,128)(2,1)}, bf16[71,32,128]{2,1,0:T(8,128)(2,1)}, u32[]{:S(2)}, u32[]{:S(2)}) collective-permute-start(bf16[71,32,128]{2,1,0:T(8,128)(2,1)} %slice.51), channel_id=1, source_target_pairs={{0,224},{8,232},{16,240},{24,248},{32,0},{40,8},{48,16},{56,24},{6... | collective-permute-start | bytes 1744904 | tf_op jit(solution)/shard_map/ppermute | solution.py:196
  124.8 10.1 %collective-permute-start.28 = (bf16[33,32,128]{2,1,0:T(8,128)(2,1)}, bf16[33,32,128]{2,1,0:T(8,128)(2,1)}, u32[]{:S(2)}, u32[]{:S(2)}) collective-permute-start(bf16[33,32,128]{2,1,0:T(8,128)(2,1)} %slice.50), channel_id=1, source_target_pairs={{0,32},{8,40},{16,48},{24,56},{32,64},{40,72},{48,80},{56,88},{64,... | collective-permute-start | bytes 811016 | tf_op jit(solution)/shard_map/ppermute | solution.py:196
  162.5 33.9 %all-to-all-start = ((bf16[32,32,256]{2,1,0:T(8,128)(2,1)}), bf16[32,32,256]{2,1,0:T(8,128)(2,1)S(1)}, u32[]{:S(2)}, u32[]{:S(2)}) async-start(bf16[32,32,256]{2,1,0:T(8,128)(2,1)} %column.1), calls=%async_computation | async-start | bytes 1048576 | tf_op jit(solution)/shard_map/all_to_all | solution.py:349
  170.8 12.8 %collective-permute-start.30 = (bf16[4,32,1024]{2,1,0:T(8,128)(2,1)}, bf16[4,32,1024]{2,1,0:T(8,128)(2,1)S(1)}, u32[]{:S(2)}, u32[]{:S(2)}) collective-permute-start(bf16[4,32,1024]{2,1,0:T(8,128)(2,1)} %copy-done.9), channel_id=1, source_target_pairs={{0,1},{1,0},{2,3},{3,2},{4,5},{5,4},{6,7},{7,6},{8,9},{9,8},{10,11... | collective-permute-start | bytes 786440 | tf_op jit(solution)/shard_map/ppermute | solution.py:264
  183.6 12.7 %collective-permute-start.33 = (bf16[64,1024]{1,0:T(8,128)(2,1)S(1)}, bf16[64,1024]{1,0:T(8,128)(2,1)S(1)}, u32[]{:S(2)}, u32[]{:S(2)}) collective-permute-start(bf16[64,1024]{1,0:T(8,128)(2,1)S(1)} %pad_maximum_fusion.4), channel_id=1, source_target_pairs={{0,6},{1,7},{2,0},{3,1},{4,2},{5,3},{6,4},{7,5},{8,14},{9,15},{10,... | collective-permute-start | bytes 393224 | tf_op jit(solution)/shard_map/ppermute | solution.py:264
  186.5 9.8 %collective-permute-start.32 = (bf16[64,1024]{1,0:T(8,128)(2,1)S(1)}, bf16[64,1024]{1,0:T(8,128)(2,1)S(1)}, u32[]{:S(2)}, u32[]{:S(2)}) collective-permute-start(bf16[64,1024]{1,0:T(8,128)(2,1)S(1)} %pad_maximum_fusion.3), channel_id=1, source_target_pairs={{0,4},{1,5},{2,6},{3,7},{4,0},{5,1},{6,2},{7,3},{8,12},{9,13},{10,... | collective-permute-start | bytes 393224 | tf_op jit(solution)/shard_map/ppermute | solution.py:264
  186.9 9.4 %collective-permute-start.31 = (bf16[64,1024]{1,0:T(8,128)(2,1)S(1)}, bf16[64,1024]{1,0:T(8,128)(2,1)S(1)}, u32[]{:S(2)}, u32[]{:S(2)}) collective-permute-start(bf16[64,1024]{1,0:T(8,128)(2,1)S(1)} %pad_maximum_fusion.2), channel_id=1, source_target_pairs={{0,2},{1,3},{2,4},{3,5},{4,6},{5,7},{6,0},{7,1},{8,10},{9,11},{10,... | collective-permute-start | bytes 393224 | tf_op jit(solution)/shard_map/ppermute | solution.py:264
  197.1 9.0 %all-to-all-start.1 = ((bf16[8,32,256]{2,1,0:T(8,128)(2,1)}), bf16[8,32,256]{2,1,0:T(8,128)(2,1)S(1)}, u32[]{:S(2)}, u32[]{:S(2)}) async-start(bf16[8,32,256]{2,1,0:T(8,128)(2,1)} %broadcast_in_dim.2), calls=%async_computation.1 | async-start | bytes 262144 | tf_op jit(solution)/shard_map/all_to_all | solution.py:314
  (16 other events, 54.3 us)
where the time goes:
time: 208 us; the launch traced here: 207 us
  waiting for transfers between devices  88.8 us (43%)
  starting transfers between devices  74.1 us (36%)
  Pallas kernels  19.2 us (9%)
  local copies, waits for them, and re-layouts  18.7 us (9%)
  other arithmetic  3.18 us (2%)
    ppermute x30, waiting for transfers between devices, hop(): blocks = lax.ppermute(piece.blocks, 'node', pairs)  71.5 us
    ppermute x30, starting transfers between devices, hop(): blocks = lax.ppermute(piece.blocks, 'node', pairs)  40.7 us
    ppermute x8, starting transfers between devices, over_feat(): return lax.ppermute(value, 'feat', pairs)  21.3 us
    ppermute x8, waiting for transfers between devices, over_feat(): return lax.ppermute(value, 'feat', pairs)  14 us
    pallas_call x1, Pallas kernels, gathered_sum(): pl.pallas_call(functools.partial(gather_kernel, [p.runs for p in pieces])...  12.3 us
    unnamed x58, local copies, waits for them, and re-layouts  10.5 us
    all_to_all x1, starting transfers between devices, per_device(): lax.all_to_all(column_for_all(acts, flat, nodes, scale), 'node', 0, 0, ti...  8.29 us
  transfers between devices with their start and end apart: 40, of which 13 were waited for; matrix products, arithmetic and copies ran while one was open for 7% of the time, Pallas kernels for 7%

commit v1 on v0

--- a/solution.py
+++ b/solution.py
@@ -15,9 +15,9 @@
 GROUPS = [("gb", (1,), True), ("gc", (2,), False), ("gd", (3, 4), True)]
 UPPER = 33
 
-QUAD = 4
+QUAD = 8
 GROUP = 8
-DEPTH = 4
+DEPTH = 3
 
 
 def plan_kernel(counts, work, length):
@@ -265,21 +265,14 @@
 
 
 def column_kernel(scale, *refs):
-    acts, flat, out, held, sems = refs[:-4], refs[-4], refs[-3], refs[-2], refs[-1]
+    acts, flat, out = refs[:-2], refs[-2], refs[-1]
     nodes = acts[0].shape[2]
     total = None
-    loads = [
-        pltpu.make_async_copy(pair, held.at[s], sems.at[s]) for s, pair in enumerate(acts)
-    ]
-    for load in loads:
-        load.start()
     for s in range(len(acts) * acts[0].shape[0]):
         pair, c = s // acts[0].shape[0], s % acts[0].shape[0]
-        if c == 0:
-            loads[pair].wait()
         term = lax.dot_general(
             flat[:, s * nodes : (s + 1) * nodes],
-            held[pair, c],
+            acts[pair][c],
             (((1,), (1,)), ((), ())),
             preferred_element_type=jnp.float32,
         )
@@ -295,12 +288,8 @@
     return pl.pallas_call(
         functools.partial(column_kernel, scale),
         out_shape=jax.ShapeDtypeStruct((copies, flat.shape[0], features), jnp.bfloat16),
-        in_specs=[pl.BlockSpec(memory_space=pl.ANY)] * len(acts) + [vmem],
+        in_specs=[vmem] * (len(acts) + 1),
         out_specs=vmem,
-        scratch_shapes=[
-            pltpu.VMEM((len(acts), *acts[0].shape), acts[0].dtype),
-            pltpu.SemaphoreType.DMA((len(acts),)),
-        ],
         compiler_params=pltpu.CompilerParams(vmem_limit_bytes=16 * 1024 * 1024),
         cost_estimate=pl.CostEstimate(
             flops=2 * features * flat.size, bytes_accessed=2 * features * flat.shape[1], transcendentals=0

time: 208 us -> 207 us (level)
  Pallas kernels: 19.2 us -> 21.3 us
  waiting for transfers between devices: 88.8 us -> 86.7 us
    pallas_call x1, Pallas kernels: 12.3 us -> 14.6 us  [gathered_sum(): pl.pallas_call(functools.partial(gather_kernel, [p.runs for p in pieces])...]
    ppermute x8, waiting for transfers between devices: 14 us -> 11.9 us  [over_feat(): return lax.ppermute(value, 'feat', pairs)]
  transfers between devices with their start and end apart: 40 -> 40, of which waited for: 13 -> 13; matrix products, arithmetic and copies ran while one was open for 7% -> 7% of each run, Pallas kernels for 7% -> 8%
where the time goes in v1:
time: 207 us; the launch traced here: 206 us
  waiting for transfers between devices  86.7 us (42%)
  starting transfers between devices  73.5 us (36%)
  Pallas kernels  21.3 us (10%)
  local copies, waits for them, and re-layouts  18.7 us (9%)
  other arithmetic  3.18 us (2%)
    ppermute x30, waiting for transfers between devices, hop(): blocks = lax.ppermute(piece.blocks, 'node', pairs)  71.5 us
    ppermute x30, starting transfers between devices, hop(): blocks = lax.ppermute(piece.blocks, 'node', pairs)  40.7 us
    ppermute x8, starting transfers between devices, over_feat(): return lax.ppermute(value, 'feat', pairs)  21.3 us
    pallas_call x1, Pallas kernels, gathered_sum(): pl.pallas_call(functools.partial(gather_kernel, [p.runs for p in pieces])...  14.6 us
    ppermute x8, waiting for transfers between devices, over_feat(): return lax.ppermute(value, 'feat', pairs)  11.9 us
    unnamed x58, local copies, waits for them, and re-layouts  10.5 us
    all_to_all x1, starting transfers between devices, per_device(): lax.all_to_all(column_for_all(acts, flat, nodes, scale), 'node', 0, 0, ti...  7.67 us
  transfers between devices with their start and end apart: 40, of which 13 were waited for; matrix products, arithmetic and copies ran while one was open for 7% of the time, Pallas kernels for 8%

profile of v1, /device:TPU:1, one launch (start us, length us, event | category | flops | bytes accessed | tf_op | source)
XLA Modules:
  0.0 206.4 jit_solution(8651555095762198548)
XLA Ops:
  0.6 1.4 bitcast_bitcast_fusion
  2.0 2.1 %collective-permute-start = (bf16[26,32,128]{2,1,0:T(8,128)(2,1)S(1)}, bf16[26,32,128]{2,1,0:T(8,128)(2,1)S(1)}, u32[]{:S(2)}, u32[]{:S(2)}) collective-permute-start(bf16[26,32,128]{2,1,0:T(8,128)(2,1)S(1)} %slice.49), channel_id=1, source_target_pairs={{0,8},{8,16},{16,24},{24,0},{32,40},{40,48},{48,56},{56,32},{64,72... | collective-permute-start | bytes 638984 | tf_op jit(solution)/shard_map/ppermute | solution.py:196
  4.2 1.7 collective-permute-start.3
  5.9 1.5 collective-permute-start.1
  7.3 1.3 collective-permute-done
  8.6 1.4 collective-permute-start.2
  10.0 5.8 %collective-permute-start.4 = (bf16[38,32,128]{2,1,0:T(8,128)(2,1)S(1)}, bf16[38,32,128]{2,1,0:T(8,128)(2,1)S(1)}, u32[]{:S(2)}, u32[]{:S(2)}) collective-permute-start(bf16[38,32,128]{2,1,0:T(8,128)(2,1)S(1)} %slice.48.rest_0_), channel_id=1, source_target_pairs={{0,224},{8,232},{16,240},{24,248},{32,0},{40,8},{48,16},{56,24},{6... | collective-permute-start | bytes 933896 | tf_op jit(solution)/shard_map/ppermute | solution.py:196
  15.9 2.1 %collective-permute-start.34 = (bf16[256,1024]{1,0:T(8,128)(2,1)}, bf16[256,1024]{1,0:T(8,128)(2,1)S(1)}, u32[]{:S(2)}, u32[]{:S(2)}) collective-permute-start(bf16[256,1024]{1,0:T(8,128)(2,1)} %param.9), channel_id=1, source_target_pairs={{0,1},{1,0},{2,3},{3,2},{4,5},{5,4},{6,7},{7,6},{8,9},{9,8},{10,11... | collective-permute-start | bytes 1572872 | tf_op jit(solution)/shard_map/ppermute | solution.py:264
  17.9 2.7 %collective-permute-start.11 = (bf16[38,32,128]{2,1,0:T(8,128)(2,1)S(1)}, bf16[38,32,128]{2,1,0:T(8,128)(2,1)S(1)}, u32[]{:S(2)}, u32[]{:S(2)}) collective-permute-start(bf16[38,32,128]{2,1,0:T(8,128)(2,1)S(1)} %slice.48.rest_0_), channel_id=1, source_target_pairs={{0,24},{8,0},{16,8},{24,16},{32,56},{40,32},{48,40},{56,48},{64,88... | collective-permute-start | bytes 933896 | tf_op jit(solution)/shard_map/ppermute | solution.py:196
  20.9 3.3 %collective-permute-start.23 = (bf16[104,32,128]{2,1,0:T(8,128)(2,1)S(1)}, bf16[104,32,128]{2,1,0:T(8,128)(2,1)S(1)}, u32[]{:S(2)}, u32[]{:S(2)}) collective-permute-start(bf16[104,32,128]{2,1,0:T(8,128)(2,1)S(1)} %pad_maximum_fusion.1.rest_1_), channel_id=1, source_target_pairs={{0,224},{8,232},{16,240},{24,248},{32,0},{40,8},{48,16},{56,24},{6... | collective-permute-start | bytes 2555912 | tf_op jit(solution)/shard_map/ppermute | solution.py:196
  24.2 3.2 %collective-permute-done.11.rest_6_ = bf16[38,32,128]{2,1,0:T(8,128)(2,1)S(1)} collective-permute-done((bf16[38,32,128]{2,1,0:T(8,128)(2,1)S(1)}, bf16[38,32,128]{2,1,0:T(8,128)(2,1)S(1)}, u32[]{:S(2)}, u32[]{:S(2)}) %collective-permute-start.11) | collective-permute-done | bytes 311328 | tf_op jit(solution)/shard_map/ppermute | solution.py:196
  28.1 2.4 %collective-permute-done.10.rest_5_ = bf16[38,32,128]{2,1,0:T(8,128)(2,1)S(1)} collective-permute-done((bf16[38,32,128]{2,1,0:T(8,128)(2,1)S(1)}, bf16[38,32,128]{2,1,0:T(8,128)(2,1)S(1)}, u32[]{:S(2)}, u32[]{:S(2)}) %collective-permute-start.10) | collective-permute-done | bytes 311328 | tf_op jit(solution)/shard_map/ppermute | solution.py:196
  30.5 1.0 collective-permute-start.12
  32.4 14.1 %collective-permute-done.6 = bf16[38,32,128]{2,1,0:T(8,128)(2,1)S(1)} collective-permute-done((bf16[38,32,128]{2,1,0:T(8,128)(2,1)S(1)}, bf16[38,32,128]{2,1,0:T(8,128)(2,1)S(1)}, u32[]{:S(2)}, u32[]{:S(2)}) %collective-permute-start.6) | collective-permute-done | bytes 311328 | tf_op jit(solution)/shard_map/ppermute | solution.py:196
  46.5 1.2 collective-permute-start.13
  48.4 1.5 collective-permute-start.14
  49.9 3.4 %collective-permute-start.8 = (bf16[38,32,128]{2,1,0:T(8,128)(2,1)S(1)}, bf16[38,32,128]{2,1,0:T(8,128)(2,1)S(1)}, u32[]{:S(2)}, u32[]{:S(2)}) collective-permute-start(bf16[38,32,128]{2,1,0:T(8,128)(2,1)S(1)} %collective-permute-done.6), channel_id=1, source_target_pairs={{0,224},{8,232},{16,240},{24,248},{32,0},{40,8},{48,16},{56,24},{6... | collective-permute-start | bytes 933896 | tf_op jit(solution)/shard_map/ppermute | solution.py:196
  53.4 3.8 %collective-permute-done.8 = bf16[38,32,128]{2,1,0:T(8,128)(2,1)S(1)} collective-permute-done((bf16[38,32,128]{2,1,0:T(8,128)(2,1)S(1)}, bf16[38,32,128]{2,1,0:T(8,128)(2,1)S(1)}, u32[]{:S(2)}, u32[]{:S(2)}) %collective-permute-start.8) | collective-permute-done | bytes 311328 | tf_op jit(solution)/shard_map/ppermute | solution.py:196
  57.2 1.5 collective-permute-start.17
  58.6 3.4 %collective-permute-start.25 = (bf16[104,32,128]{2,1,0:T(8,128)(2,1)S(1)}, bf16[104,32,128]{2,1,0:T(8,128)(2,1)S(1)}, u32[]{:S(2)}, u32[]{:S(2)}) collective-permute-start(bf16[104,32,128]{2,1,0:T(8,128)(2,1)S(1)} %collective-permute-done.23.rest_18_), channel_id=1, source_target_pairs={{0,224},{8,232},{16,240},{24,248},{32,0},{40,8},{48,16},{56,24},{6... | collective-permute-start | bytes 2555912 | tf_op jit(solution)/shard_map/ppermute | solution.py:196
  62.3 6.7 %collective-permute-done.9 = bf16[38,32,128]{2,1,0:T(8,128)(2,1)S(1)} collective-permute-done((bf16[38,32,128]{2,1,0:T(8,128)(2,1)S(1)}, bf16[38,32,128]{2,1,0:T(8,128)(2,1)S(1)}, u32[]{:S(2)}, u32[]{:S(2)}) %collective-permute-start.9) | collective-permute-done | bytes 311328 | tf_op jit(solution)/shard_map/ppermute | solution.py:196
  69.1 4.6 %collective-permute-done.17.rest_12_ = bf16[76,32,128]{2,1,0:T(8,128)(2,1)S(1)} collective-permute-done((bf16[76,32,128]{2,1,0:T(8,128)(2,1)S(1)}, bf16[76,32,128]{2,1,0:T(8,128)(2,1)S(1)}, u32[]{:S(2)}, u32[]{:S(2)}) %collective-permute-start.17) | collective-permute-done | bytes 622624 | tf_op jit(solution)/shard_map/ppermute | solution.py:196
  74.6 1.8 collective-permute-start.20
  76.4 3.4 %collective-permute-start.27 = (bf16[104,32,128]{2,1,0:T(8,128)(2,1)S(1)}, bf16[104,32,128]{2,1,0:T(8,128)(2,1)S(1)}, u32[]{:S(2)}, u32[]{:S(2)}) collective-permute-start(bf16[104,32,128]{2,1,0:T(8,128)(2,1)S(1)} %collective-permute-done.25.rest_20_), channel_id=1, source_target_pairs={{0,224},{8,232},{16,240},{24,248},{32,0},{40,8},{48,16},{56,24},{6... | collective-permute-start | bytes 2555912 | tf_op jit(solution)/shard_map/ppermute | solution.py:196
  79.8 6.0 %collective-permute-done.15.rest_10_ = bf16[76,32,128]{2,1,0:T(8,128)(2,1)S(1)} collective-permute-done((bf16[76,32,128]{2,1,0:T(8,128)(2,1)S(1)}, bf16[76,32,128]{2,1,0:T(8,128)(2,1)S(1)}, u32[]{:S(2)}, u32[]{:S(2)}) %collective-permute-start.15) | collective-permute-done | bytes 622624 | tf_op jit(solution)/shard_map/ppermute | solution.py:196
  86.6 19.1 %collective-permute-done.19.rest_14_ = bf16[114,32,128]{2,1,0:T(8,128)(2,1)S(1)} collective-permute-done((bf16[114,32,128]{2,1,0:T(8,128)(2,1)S(1)}, bf16[114,32,128]{2,1,0:T(8,128)(2,1)S(1)}, u32[]{:S(2)}, u32[]{:S(2)}) %collective-permute-start.19) | collective-permute-done | bytes 933920 | tf_op jit(solution)/shard_map/ppermute | solution.py:196
  105.7 1.5 pad_maximum_fusion.refs_0_
  107.2 2.8 %collective-permute-start.35 = (bf16[2,256,1024]{2,1,0:T(8,128)(2,1)S(1)}, bf16[2,256,1024]{2,1,0:T(8,128)(2,1)}, u32[]{:S(2)}, u32[]{:S(2)}) collective-permute-start(bf16[2,256,1024]{2,1,0:T(8,128)(2,1)S(1)} %pad_maximum_fusion.refs_0_), channel_id=1, source_target_pairs={{0,6},{1,7},{2,0},{3,1},{4,2},{5,3},{6,4},{7,5},{8,14},{9,15},{10,... | collective-permute-start | bytes 3145736 | tf_op jit(solution)/shard_map/ppermute | solution.py:264
  110.4 1.0 collective-permute-start.37
  112.2 1.4 collective-permute-start.29
  114.4 10.4 %collective-permute-done.21.rest_16_ = bf16[114,32,128]{2,1,0:T(8,128)(2,1)S(1)} collective-permute-done((bf16[114,32,128]{2,1,0:T(8,128)(2,1)S(1)}, bf16[114,32,128]{2,1,0:T(8,128)(2,1)S(1)}, u32[]{:S(2)}, u32[]{:S(2)}) %collective-permute-start.21) | collective-permute-done | bytes 933920 | tf_op jit(solution)/shard_map/ppermute | solution.py:196
  125.8 2.7 %plan.1 = (s32[200]{0:T(256)}, s32[1]{0:T(128)}) custom-call(s32[64]{0:T(128)} %counts.3), custom_call_target="tpu_custom_call" | custom-call | tf_op jit(solution)/shard_map/plan/pallas_call | solution.py:44
  128.5 1.4 copy.9
  130.8 2.1 %constant_dynamic-slice_fusion = (bf16[256,32]{1,0:T(8,128)(2,1)}, bf16[256,32]{1,0:T(8,128)(2,1)}, bf16[256,32]{1,0:T(8,128)(2,1)}, bf16[256,32]{1,0:T(8,128)(2...) fusion(bf16[256,256]{1,0:T(8,128)(2,1)} %param.10, ...), kind=kLoop, calls=%fused_computation.29 | loop fusion | bytes 262176 | tf_op jit(solution)/shard_map/dynamic_slice | solution.py:324
  132.8 1.9 concatenate.27
  134.8 1.1 copy-done.1
  135.9 1.0 copy-done.3
  136.9 1.0 copy-done.5
  139.1 14.6 %gathered_sum.1 = (bf16[4,32,1024]{2,1,0:T(8,128)(2,1)S(1)}, bf16[4,32,1024]{2,1,0:T(8,128)(2,1)S(1)}, bf16[32,8192]{1,0:T(8,128)(2,1)S(1)}) custom-call(s32[4]{0:T(128)S(1)} %pad_add_fusion.here, s32[200]{0:T(256)S(1)} %copy-done.7, s32[1]{0:T(128)} %get-tuple-element.8.length, s32[64]{0:T(128)S(1)} %copy-done.8, s32[1536]{0:T(1024)S(1)} %reshape.17.indices, ...), custom_call_target="tpu_custom_call" | custom-call | flops 805306368 | bytes 41943040 | tf_op jit(solution)/shard_map/gathered_sum/pallas_call | solution.py:158
  155.2 3.3 %collective-permute-done.37.refs_3_ = bf16[2,256,1024]{2,1,0:T(8,128)(2,1)} collective-permute-done((bf16[2,256,1024]{2,1,0:T(8,128)(2,1)S(1)}, bf16[2,256,1024]{2,1,0:T(8,128)(2,1)}, u32[]{:S(2)}, u32[]{:S(2)}) %collective-permute-start.37) | collective-permute-done | bytes 1048608 | tf_op jit(solution)/shard_map/ppermute | solution.py:264
  158.4 4.0 %column.1 = bf16[32,32,256]{2,1,0:T(8,128)(2,1)} custom-call(bf16[2,256,1024]{2,1,0:T(8,128)(2,1)S(1)} %pad_maximum_fusion.refs_0_, bf16[2,256,1024]{2,1,0:T(8,128)(2,1)} %collective-permute-done.35.refs_1_, bf16[2,256,1024]{2,1,0:T(8,128)(2,1)} %collective-permute-done.36.refs_2_, bf16[2,256,1024]{2,1,0:T(8,128)(2,1)} %collective-permute-done.37.refs_3_, ...), custom_call_target="tpu_custom_call" | custom-call | flops 134217728 | bytes 4194304 | tf_op jit(solution)/shard_map/column/pallas_call | solution.py:288
  162.5 7.7 %all-to-all-start = ((bf16[32,32,256]{2,1,0:T(8,128)(2,1)}), bf16[32,32,256]{2,1,0:T(8,128)(2,1)S(1)}, u32[]{:S(2)}, u32[]{:S(2)}) async-start(bf16[32,32,256]{2,1,0:T(8,128)(2,1)} %column.1), calls=%async_computation | async-start | bytes 1048576 | tf_op jit(solution)/shard_map/all_to_all | solution.py:338
  170.2 11.1 %collective-permute-start.30 = (bf16[4,32,1024]{2,1,0:T(8,128)(2,1)}, bf16[4,32,1024]{2,1,0:T(8,128)(2,1)S(1)}, u32[]{:S(2)}, u32[]{:S(2)}) collective-permute-start(bf16[4,32,1024]{2,1,0:T(8,128)(2,1)} %copy-done.9), channel_id=1, source_target_pairs={{0,1},{1,0},{2,3},{3,2},{4,5},{5,4},{6,7},{7,6},{8,9},{9,8},{10,11... | collective-permute-start | bytes 786440 | tf_op jit(solution)/shard_map/ppermute | solution.py:264
  183.0 2.8 %collective-permute-start.33 = (bf16[64,1024]{1,0:T(8,128)(2,1)S(1)}, bf16[64,1024]{1,0:T(8,128)(2,1)S(1)}, u32[]{:S(2)}, u32[]{:S(2)}) collective-permute-start(bf16[64,1024]{1,0:T(8,128)(2,1)S(1)} %pad_maximum_fusion.4), channel_id=1, source_target_pairs={{0,6},{1,7},{2,0},{3,1},{4,2},{5,3},{6,4},{7,5},{8,14},{9,15},{10,... | collective-permute-start | bytes 393224 | tf_op jit(solution)/shard_map/ppermute | solution.py:264
  187.1 8.6 %collective-permute-done.31 = bf16[64,1024]{1,0:T(8,128)(2,1)S(1)} collective-permute-done((bf16[64,1024]{1,0:T(8,128)(2,1)S(1)}, bf16[64,1024]{1,0:T(8,128)(2,1)S(1)}, u32[]{:S(2)}, u32[]{:S(2)}) %collective-permute-start.31) | collective-permute-done | bytes 131104 | tf_op jit(solution)/shard_map/ppermute | solution.py:264
  196.5 3.8 %all-to-all-start.1 = ((bf16[8,32,256]{2,1,0:T(8,128)(2,1)}), bf16[8,32,256]{2,1,0:T(8,128)(2,1)S(1)}, u32[]{:S(2)}, u32[]{:S(2)}) async-start(bf16[8,32,256]{2,1,0:T(8,128)(2,1)} %broadcast_in_dim.2), calls=%async_computation.1 | async-start | bytes 262144 | tf_op jit(solution)/shard_map/all_to_all | solution.py:303
  200.3 2.0 convolution_convert_fusion
  202.3 3.3 %all-to-all-done.1 = bf16[8,32,256]{2,1,0:T(8,128)(2,1)S(1)} async-done(((bf16[8,32,256]{2,1,0:T(8,128)(2,1)}), bf16[8,32,256]{2,1,0:T(8,128)(2,1)S(1)}, u32[]{:S(2)}, u32[]{:S(2)}) %all-to-all-start.1) | async-done | bytes 131104 | tf_op jit(solution)/shard_map/all_to_all | solution.py:303
  (117 shorter events, 15.9 us)
Async XLA Ops:
  2.0 6.6 %collective-permute-start = (bf16[26,32,128]{2,1,0:T(8,128)(2,1)S(1)}, bf16[26,32,128]{2,1,0:T(8,128)(2,1)S(1)}, u32[]{:S(2)}, u32[]{:S(2)}) collective-permute-start(bf16[26,32,128]{2,1,0:T(8,128)(2,1)S(1)} %slice.49), channel_id=1, source_target_pairs={{0,8},{8,16},{16,24},{24,0},{32,40},{40,48},{48,56},{56,32},{64,72... | collective-permute-start | bytes 638984 | tf_op jit(solution)/shard_map/ppermute | solution.py:196
  4.2 16.5 %collective-permute-start.3 = (bf16[38,32,128]{2,1,0:T(8,128)(2,1)S(1)}, bf16[38,32,128]{2,1,0:T(8,128)(2,1)S(1)}, u32[]{:S(2)}, u32[]{:S(2)}) collective-permute-start(bf16[38,32,128]{2,1,0:T(8,128)(2,1)S(1)} %slice.48.rest_0_), channel_id=1, source_target_pairs={{0,32},{8,40},{16,48},{24,56},{32,64},{40,72},{48,80},{56,88},{64,... | collective-permute-start | bytes 933896 | tf_op jit(solution)/shard_map/ppermute | solution.py:196
  5.9 12.1 %collective-permute-start.1 = (bf16[26,32,128]{2,1,0:T(8,128)(2,1)S(1)}, bf16[26,32,128]{2,1,0:T(8,128)(2,1)S(1)}, u32[]{:S(2)}, u32[]{:S(2)}) collective-permute-start(bf16[26,32,128]{2,1,0:T(8,128)(2,1)S(1)} %slice.49), channel_id=1, source_target_pairs={{0,24},{8,0},{16,8},{24,16},{32,56},{40,32},{48,40},{56,48},{64,88... | collective-permute-start | bytes 638984 | tf_op jit(solution)/shard_map/ppermute | solution.py:196
  8.6 12.0 %collective-permute-start.2 = (bf16[26,32,128]{2,1,0:T(8,128)(2,1)S(1)}, bf16[26,32,128]{2,1,0:T(8,128)(2,1)S(1)}, u32[]{:S(2)}, u32[]{:S(2)}) collective-permute-start(bf16[26,32,128]{2,1,0:T(8,128)(2,1)S(1)} %collective-permute-done), channel_id=1, source_target_pairs={{0,8},{8,16},{16,24},{24,0},{32,40},{40,48},{48,56},{56,32},{64,72... | collective-permute-start | bytes 638984 | tf_op jit(solution)/shard_map/ppermute | solution.py:196
  10.0 10.8 %collective-permute-start.4 = (bf16[38,32,128]{2,1,0:T(8,128)(2,1)S(1)}, bf16[38,32,128]{2,1,0:T(8,128)(2,1)S(1)}, u32[]{:S(2)}, u32[]{:S(2)}) collective-permute-start(bf16[38,32,128]{2,1,0:T(8,128)(2,1)S(1)} %slice.48.rest_0_), channel_id=1, source_target_pairs={{0,224},{8,232},{16,240},{24,248},{32,0},{40,8},{48,16},{56,24},{6... | collective-permute-start | bytes 933896 | tf_op jit(solution)/shard_map/ppermute | solution.py:196
  15.9 16.4 %collective-permute-start.34 = (bf16[256,1024]{1,0:T(8,128)(2,1)}, bf16[256,1024]{1,0:T(8,128)(2,1)S(1)}, u32[]{:S(2)}, u32[]{:S(2)}) collective-permute-start(bf16[256,1024]{1,0:T(8,128)(2,1)} %param.9), channel_id=1, source_target_pairs={{0,1},{1,0},{2,3},{3,2},{4,5},{5,4},{6,7},{7,6},{8,9},{9,8},{10,11... | collective-permute-start | bytes 1572872 | tf_op jit(solution)/shard_map/ppermute | solution.py:264
  17.9 9.4 %collective-permute-start.11 = (bf16[38,32,128]{2,1,0:T(8,128)(2,1)S(1)}, bf16[38,32,128]{2,1,0:T(8,128)(2,1)S(1)}, u32[]{:S(2)}, u32[]{:S(2)}) collective-permute-start(bf16[38,32,128]{2,1,0:T(8,128)(2,1)S(1)} %slice.48.rest_0_), channel_id=1, source_target_pairs={{0,24},{8,0},{16,8},{24,16},{32,56},{40,32},{48,40},{56,48},{64,88... | collective-permute-start | bytes 933896 | tf_op jit(solution)/shard_map/ppermute | solution.py:196
  20.6 9.8 %collective-permute-start.10 = (bf16[38,32,128]{2,1,0:T(8,128)(2,1)S(1)}, bf16[38,32,128]{2,1,0:T(8,128)(2,1)S(1)}, u32[]{:S(2)}, u32[]{:S(2)}) collective-permute-start(bf16[38,32,128]{2,1,0:T(8,128)(2,1)S(1)} %slice.48.rest_0_), channel_id=1, source_target_pairs={{0,8},{8,16},{16,24},{24,0},{32,40},{40,48},{48,56},{56,32},{64,72... | collective-permute-start | bytes 933896 | tf_op jit(solution)/shard_map/ppermute | solution.py:196
  20.6 10.8 %collective-permute-start.5 = (bf16[38,32,128]{2,1,0:T(8,128)(2,1)S(1)}, bf16[38,32,128]{2,1,0:T(8,128)(2,1)S(1)}, u32[]{:S(2)}, u32[]{:S(2)}) collective-permute-start(bf16[38,32,128]{2,1,0:T(8,128)(2,1)S(1)} %collective-permute-done.3), channel_id=1, source_target_pairs={{0,32},{8,40},{16,48},{24,56},{32,64},{40,72},{48,80},{56,88},{64,... | collective-permute-start | bytes 933896 | tf_op jit(solution)/shard_map/ppermute | solution.py:196
  20.8 89.5 %copy-start.10 = (bf16[104,32,128]{2,1,0:T(8,128)(2,1)}, bf16[104,32,128]{2,1,0:T(8,128)(2,1)S(1)}, u32[]{:S(2)}) copy-start(bf16[104,32,128]{2,1,0:T(8,128)(2,1)S(1)} %pad_maximum_fusion.1.rest_1_) | copy-start | bytes 2555908
  20.9 37.8 %collective-permute-start.23 = (bf16[104,32,128]{2,1,0:T(8,128)(2,1)S(1)}, bf16[104,32,128]{2,1,0:T(8,128)(2,1)S(1)}, u32[]{:S(2)}, u32[]{:S(2)}) collective-permute-start(bf16[104,32,128]{2,1,0:T(8,128)(2,1)S(1)} %pad_maximum_fusion.1.rest_1_), channel_id=1, source_target_pairs={{0,224},{8,232},{16,240},{24,248},{32,0},{40,8},{48,16},{56,24},{6... | collective-permute-start | bytes 2555912 | tf_op jit(solution)/shard_map/ppermute | solution.py:196
  27.3 19.1 %collective-permute-start.6 = (bf16[38,32,128]{2,1,0:T(8,128)(2,1)S(1)}, bf16[38,32,128]{2,1,0:T(8,128)(2,1)S(1)}, u32[]{:S(2)}, u32[]{:S(2)}) collective-permute-start(bf16[38,32,128]{2,1,0:T(8,128)(2,1)S(1)} %collective-permute-done.4), channel_id=1, source_target_pairs={{0,224},{8,232},{16,240},{24,248},{32,0},{40,8},{48,16},{56,24},{6... | collective-permute-start | bytes 933896 | tf_op jit(solution)/shard_map/ppermute | solution.py:196
  30.5 17.2 %collective-permute-start.12 = (bf16[38,32,128]{2,1,0:T(8,128)(2,1)S(1)}, bf16[38,32,128]{2,1,0:T(8,128)(2,1)S(1)}, u32[]{:S(2)}, u32[]{:S(2)}) collective-permute-start(bf16[38,32,128]{2,1,0:T(8,128)(2,1)S(1)} %collective-permute-done.11.rest_6_), channel_id=1, source_target_pairs={{0,24},{8,0},{16,8},{24,16},{32,56},{40,32},{48,40},{56,48},{64,88... | collective-permute-start | bytes 933896 | tf_op jit(solution)/shard_map/ppermute | solution.py:196
  31.5 18.4 %collective-permute-start.7 = (bf16[38,32,128]{2,1,0:T(8,128)(2,1)S(1)}, bf16[38,32,128]{2,1,0:T(8,128)(2,1)S(1)}, u32[]{:S(2)}, u32[]{:S(2)}) collective-permute-start(bf16[38,32,128]{2,1,0:T(8,128)(2,1)S(1)} %collective-permute-done.5), channel_id=1, source_target_pairs={{0,32},{8,40},{16,48},{24,56},{32,64},{40,72},{48,80},{56,88},{64,... | collective-permute-start | bytes 933896 | tf_op jit(solution)/shard_map/ppermute | solution.py:196
  32.3 29.9 %collective-permute-start.22 = (bf16[104,32,128]{2,1,0:T(8,128)(2,1)S(1)}, bf16[104,32,128]{2,1,0:T(8,128)(2,1)S(1)}, u32[]{:S(2)}, u32[]{:S(2)}) collective-permute-start(bf16[104,32,128]{2,1,0:T(8,128)(2,1)S(1)} %pad_maximum_fusion.1.rest_1_), channel_id=1, source_target_pairs={{0,32},{8,40},{16,48},{24,56},{32,64},{40,72},{48,80},{56,88},{64,... | collective-permute-start | bytes 2555912 | tf_op jit(solution)/shard_map/ppermute | solution.py:196
  46.5 15.6 %collective-permute-start.13 = (bf16[76,32,128]{2,1,0:T(8,128)(2,1)S(1)}, bf16[76,32,128]{2,1,0:T(8,128)(2,1)S(1)}, u32[]{:S(2)}, u32[]{:S(2)}) collective-permute-start(bf16[76,32,128]{2,1,0:T(8,128)(2,1)S(1)} %constant_dynamic-update-slice_fusion.rest_2_), channel_id=1, source_target_pairs={{0,8},{8,16},{16,24},{24,0},{32,40},{40,48},{48,56},{56,32},{64,72... | collective-permute-start | bytes 1867784 | tf_op jit(solution)/shard_map/ppermute | solution.py:196
  48.4 13.6 %collective-permute-start.14 = (bf16[76,32,128]{2,1,0:T(8,128)(2,1)S(1)}, bf16[76,32,128]{2,1,0:T(8,128)(2,1)S(1)}, u32[]{:S(2)}, u32[]{:S(2)}) collective-permute-start(bf16[76,32,128]{2,1,0:T(8,128)(2,1)S(1)} %constant_dynamic-update-slice_fusion.rest_2_), channel_id=1, source_target_pairs={{0,24},{8,0},{16,8},{24,16},{32,56},{40,32},{48,40},{56,48},{64,88... | collective-permute-start | bytes 1867784 | tf_op jit(solution)/shard_map/ppermute | solution.py:196
  49.9 7.3 %collective-permute-start.8 = (bf16[38,32,128]{2,1,0:T(8,128)(2,1)S(1)}, bf16[38,32,128]{2,1,0:T(8,128)(2,1)S(1)}, u32[]{:S(2)}, u32[]{:S(2)}) collective-permute-start(bf16[38,32,128]{2,1,0:T(8,128)(2,1)S(1)} %collective-permute-done.6), channel_id=1, source_target_pairs={{0,224},{8,232},{16,240},{24,248},{32,0},{40,8},{48,16},{56,24},{6... | collective-permute-start | bytes 933896 | tf_op jit(solution)/shard_map/ppermute | solution.py:196
  57.2 16.5 %collective-permute-start.17 = (bf16[76,32,128]{2,1,0:T(8,128)(2,1)S(1)}, bf16[76,32,128]{2,1,0:T(8,128)(2,1)S(1)}, u32[]{:S(2)}, u32[]{:S(2)}) collective-permute-start(bf16[76,32,128]{2,1,0:T(8,128)(2,1)S(1)} %constant_dynamic-update-slice_fusion.2.rest_3_), channel_id=1, source_target_pairs={{0,24},{8,0},{16,8},{24,16},{32,56},{40,32},{48,40},{56,48},{64,88... | collective-permute-start | bytes 1867784 | tf_op jit(solution)/shard_map/ppermute | solution.py:196
  58.6 27.2 %copy-start.17 = (bf16[104,32,128]{2,1,0:T(8,128)(2,1)}, bf16[104,32,128]{2,1,0:T(8,128)(2,1)S(1)}, u32[]{:S(2)}) copy-start(bf16[104,32,128]{2,1,0:T(8,128)(2,1)S(1)} %collective-permute-done.23.rest_18_) | copy-start | bytes 2555908
  58.6 17.7 %collective-permute-start.25 = (bf16[104,32,128]{2,1,0:T(8,128)(2,1)S(1)}, bf16[104,32,128]{2,1,0:T(8,128)(2,1)S(1)}, u32[]{:S(2)}, u32[]{:S(2)}) collective-permute-start(bf16[104,32,128]{2,1,0:T(8,128)(2,1)S(1)} %collective-permute-done.23.rest_18_), channel_id=1, source_target_pairs={{0,224},{8,232},{16,240},{24,248},{32,0},{40,8},{48,16},{56,24},{6... | collective-permute-start | bytes 2555912 | tf_op jit(solution)/shard_map/ppermute | solution.py:196
  62.0 7.0 %collective-permute-start.9 = (bf16[38,32,128]{2,1,0:T(8,128)(2,1)S(1)}, bf16[38,32,128]{2,1,0:T(8,128)(2,1)S(1)}, u32[]{:S(2)}, u32[]{:S(2)}) collective-permute-start(bf16[38,32,128]{2,1,0:T(8,128)(2,1)S(1)} %collective-permute-done.7), channel_id=1, source_target_pairs={{0,32},{8,40},{16,48},{24,56},{32,64},{40,72},{48,80},{56,88},{64,... | collective-permute-start | bytes 933896 | tf_op jit(solution)/shard_map/ppermute | solution.py:196
  62.0 43.6 %copy-start = (bf16[76,32,128]{2,1,0:T(8,128)(2,1)}, bf16[76,32,128]{2,1,0:T(8,128)(2,1)S(1)}, u32[]{:S(2)}) copy-start(bf16[76,32,128]{2,1,0:T(8,128)(2,1)S(1)} %collective-permute-done.14.rest_9_) | copy-start | bytes 1867780
  62.1 12.5 %collective-permute-start.16 = (bf16[76,32,128]{2,1,0:T(8,128)(2,1)S(1)}, bf16[76,32,128]{2,1,0:T(8,128)(2,1)}, u32[]{:S(2)}, u32[]{:S(2)}) collective-permute-start(bf16[76,32,128]{2,1,0:T(8,128)(2,1)S(1)} %constant_dynamic-update-slice_fusion.2.rest_3_), channel_id=1, source_target_pairs={{0,8},{8,16},{16,24},{24,0},{32,40},{40,48},{48,56},{56,32},{64,72... | collective-permute-start | bytes 1867784 | tf_op jit(solution)/shard_map/ppermute | solution.py:196
  62.2 43.5 %copy-start.18 = (bf16[104,32,128]{2,1,0:T(8,128)(2,1)}, bf16[104,32,128]{2,1,0:T(8,128)(2,1)S(1)}, u32[]{:S(2)}) copy-start(bf16[104,32,128]{2,1,0:T(8,128)(2,1)S(1)} %collective-permute-done.22.rest_17_) | copy-start | bytes 2555908
  62.2 23.6 %collective-permute-start.24 = (bf16[104,32,128]{2,1,0:T(8,128)(2,1)S(1)}, bf16[104,32,128]{2,1,0:T(8,128)(2,1)S(1)}, u32[]{:S(2)}, u32[]{:S(2)}) collective-permute-start(bf16[104,32,128]{2,1,0:T(8,128)(2,1)S(1)} %collective-permute-done.22.rest_17_), channel_id=1, source_target_pairs={{0,32},{8,40},{16,48},{24,56},{32,64},{40,72},{48,80},{56,88},{64,... | collective-permute-start | bytes 2555912 | tf_op jit(solution)/shard_map/ppermute | solution.py:196
  69.0 16.8 %collective-permute-start.15 = (bf16[76,32,128]{2,1,0:T(8,128)(2,1)S(1)}, bf16[76,32,128]{2,1,0:T(8,128)(2,1)S(1)}, u32[]{:S(2)}, u32[]{:S(2)}) collective-permute-start(bf16[76,32,128]{2,1,0:T(8,128)(2,1)S(1)} %collective-permute-done.13.rest_8_), channel_id=1, source_target_pairs={{0,8},{8,16},{16,24},{24,0},{32,40},{40,48},{48,56},{56,32},{64,72... | collective-permute-start | bytes 1867784 | tf_op jit(solution)/shard_map/ppermute | solution.py:196
  69.0 43.2 %copy-start.12 = (bf16[114,32,128]{2,1,0:T(8,128)(2,1)}, bf16[114,32,128]{2,1,0:T(8,128)(2,1)S(1)}, u32[]{:S(2)}) copy-start(bf16[114,32,128]{2,1,0:T(8,128)(2,1)S(1)} %constant_dynamic-update-slice_fusion.4.rest_4_) | copy-start | bytes 2801668
  73.7 51.7 %copy-start.21 = (bf16[76,32,128]{2,1,0:T(8,128)(2,1)}, bf16[76,32,128]{2,1,0:T(8,128)(2,1)S(1)}, u32[]{:S(2)}) copy-start(bf16[76,32,128]{2,1,0:T(8,128)(2,1)S(1)} %collective-permute-done.17.rest_12_) | copy-start | bytes 1867780
  73.7 32.0 %collective-permute-start.19 = (bf16[114,32,128]{2,1,0:T(8,128)(2,1)S(1)}, bf16[114,32,128]{2,1,0:T(8,128)(2,1)S(1)}, u32[]{:S(2)}, u32[]{:S(2)}) collective-permute-start(bf16[114,32,128]{2,1,0:T(8,128)(2,1)S(1)} %constant_dynamic-update-slice_fusion.4.rest_4_), channel_id=1, source_target_pairs={{0,8},{8,16},{16,24},{24,0},{32,40},{40,48},{48,56},{56,32},{64,72... | collective-permute-start | bytes 2801672 | tf_op jit(solution)/shard_map/ppermute | solution.py:196
  74.6 35.4 %collective-permute-start.20 = (bf16[114,32,128]{2,1,0:T(8,128)(2,1)S(1)}, bf16[114,32,128]{2,1,0:T(8,128)(2,1)S(1)}, u32[]{:S(2)}, u32[]{:S(2)}) collective-permute-start(bf16[114,32,128]{2,1,0:T(8,128)(2,1)S(1)} %constant_dynamic-update-slice_fusion.4.rest_4_), channel_id=1, source_target_pairs={{0,24},{8,0},{16,8},{24,16},{32,56},{40,32},{48,40},{56,48},{64,88... | collective-permute-start | bytes 2801672 | tf_op jit(solution)/shard_map/ppermute | solution.py:196
  76.4 49.0 %copy-start.19 = (bf16[104,32,128]{2,1,0:T(8,128)(2,1)}, bf16[104,32,128]{2,1,0:T(8,128)(2,1)S(1)}, u32[]{:S(2)}) copy-start(bf16[104,32,128]{2,1,0:T(8,128)(2,1)S(1)} %collective-permute-done.25.rest_20_) | copy-start | bytes 2555908
  76.4 34.0 %collective-permute-start.27 = (bf16[104,32,128]{2,1,0:T(8,128)(2,1)S(1)}, bf16[104,32,128]{2,1,0:T(8,128)(2,1)S(1)}, u32[]{:S(2)}, u32[]{:S(2)}) collective-permute-start(bf16[104,32,128]{2,1,0:T(8,128)(2,1)S(1)} %collective-permute-done.25.rest_20_), channel_id=1, source_target_pairs={{0,224},{8,232},{16,240},{24,248},{32,0},{40,8},{48,16},{56,24},{6... | collective-permute-start | bytes 2555912 | tf_op jit(solution)/shard_map/ppermute | solution.py:196
  85.8 21.4 %collective-permute-start.18 = (bf16[76,32,128]{2,1,0:T(8,128)(2,1)S(1)}, bf16[76,32,128]{2,1,0:T(8,128)(2,1)S(1)}, u32[]{:S(2)}, u32[]{:S(2)}) collective-permute-start(bf16[76,32,128]{2,1,0:T(8,128)(2,1)S(1)} %collective-permute-done.17.rest_12_), channel_id=1, source_target_pairs={{0,24},{8,0},{16,8},{24,16},{32,56},{40,32},{48,40},{56,48},{64,88... | collective-permute-start | bytes 1867784 | tf_op jit(solution)/shard_map/ppermute | solution.py:196
  85.8 39.6 %copy-start.20 = (bf16[104,32,128]{2,1,0:T(8,128)(2,1)}, bf16[104,32,128]{2,1,0:T(8,128)(2,1)S(1)}, u32[]{:S(2)}) copy-start(bf16[104,32,128]{2,1,0:T(8,128)(2,1)S(1)} %collective-permute-done.24.rest_19_) | copy-start | bytes 2555908
  85.8 26.4 %collective-permute-start.26 = (bf16[104,32,128]{2,1,0:T(8,128)(2,1)S(1)}, bf16[104,32,128]{2,1,0:T(8,128)(2,1)S(1)}, u32[]{:S(2)}, u32[]{:S(2)}) collective-permute-start(bf16[104,32,128]{2,1,0:T(8,128)(2,1)S(1)} %collective-permute-done.24.rest_19_), channel_id=1, source_target_pairs={{0,32},{8,40},{16,48},{24,56},{32,64},{40,72},{48,80},{56,88},{64,... | collective-permute-start | bytes 2555912 | tf_op jit(solution)/shard_map/ppermute | solution.py:196
  105.7 19.2 %collective-permute-start.21 = (bf16[114,32,128]{2,1,0:T(8,128)(2,1)S(1)}, bf16[114,32,128]{2,1,0:T(8,128)(2,1)S(1)}, u32[]{:S(2)}, u32[]{:S(2)}) collective-permute-start(bf16[114,32,128]{2,1,0:T(8,128)(2,1)S(1)} %collective-permute-done.19.rest_14_), channel_id=1, source_target_pairs={{0,8},{8,16},{16,24},{24,0},{32,40},{40,48},{48,56},{56,32},{64,72... | collective-permute-start | bytes 2801672 | tf_op jit(solution)/shard_map/ppermute | solution.py:196
  107.2 48.0 %collective-permute-start.35 = (bf16[2,256,1024]{2,1,0:T(8,128)(2,1)S(1)}, bf16[2,256,1024]{2,1,0:T(8,128)(2,1)}, u32[]{:S(2)}, u32[]{:S(2)}) collective-permute-start(bf16[2,256,1024]{2,1,0:T(8,128)(2,1)S(1)} %pad_maximum_fusion.refs_0_), channel_id=1, source_target_pairs={{0,6},{1,7},{2,0},{3,1},{4,2},{5,3},{6,4},{7,5},{8,14},{9,15},{10,... | collective-permute-start | bytes 3145736 | tf_op jit(solution)/shard_map/ppermute | solution.py:264
  110.0 45.1 %collective-permute-start.36 = (bf16[2,256,1024]{2,1,0:T(8,128)(2,1)S(1)}, bf16[2,256,1024]{2,1,0:T(8,128)(2,1)}, u32[]{:S(2)}, u32[]{:S(2)}) collective-permute-start(bf16[2,256,1024]{2,1,0:T(8,128)(2,1)S(1)} %pad_maximum_fusion.refs_0_), channel_id=1, source_target_pairs={{0,4},{1,5},{2,6},{3,7},{4,0},{5,1},{6,2},{7,3},{8,12},{9,13},{10,... | collective-permute-start | bytes 3145736 | tf_op jit(solution)/shard_map/ppermute | solution.py:264
  110.4 48.1 %collective-permute-start.37 = (bf16[2,256,1024]{2,1,0:T(8,128)(2,1)S(1)}, bf16[2,256,1024]{2,1,0:T(8,128)(2,1)}, u32[]{:S(2)}, u32[]{:S(2)}) collective-permute-start(bf16[2,256,1024]{2,1,0:T(8,128)(2,1)S(1)} %pad_maximum_fusion.refs_0_), channel_id=1, source_target_pairs={{0,2},{1,3},{2,4},{3,5},{4,6},{5,7},{6,0},{7,1},{8,10},{9,11},{10,... | collective-permute-start | bytes 3145736 | tf_op jit(solution)/shard_map/ppermute | solution.py:264
  112.2 22.6 %collective-permute-start.29 = (bf16[71,32,128]{2,1,0:T(8,128)(2,1)}, bf16[71,32,128]{2,1,0:T(8,128)(2,1)}, u32[]{:S(2)}, u32[]{:S(2)}) collective-permute-start(bf16[71,32,128]{2,1,0:T(8,128)(2,1)} %slice.51), channel_id=1, source_target_pairs={{0,224},{8,232},{16,240},{24,248},{32,0},{40,8},{48,16},{56,24},{6... | collective-permute-start | bytes 1744904 | tf_op jit(solution)/shard_map/ppermute | solution.py:196
  124.8 10.0 %collective-permute-start.28 = (bf16[33,32,128]{2,1,0:T(8,128)(2,1)}, bf16[33,32,128]{2,1,0:T(8,128)(2,1)}, u32[]{:S(2)}, u32[]{:S(2)}) collective-permute-start(bf16[33,32,128]{2,1,0:T(8,128)(2,1)} %slice.50), channel_id=1, source_target_pairs={{0,32},{8,40},{16,48},{24,56},{32,64},{40,72},{48,80},{56,88},{64,... | collective-permute-start | bytes 811016 | tf_op jit(solution)/shard_map/ppermute | solution.py:196
  162.5 33.3 %all-to-all-start = ((bf16[32,32,256]{2,1,0:T(8,128)(2,1)}), bf16[32,32,256]{2,1,0:T(8,128)(2,1)S(1)}, u32[]{:S(2)}, u32[]{:S(2)}) async-start(bf16[32,32,256]{2,1,0:T(8,128)(2,1)} %column.1), calls=%async_computation | async-start | bytes 1048576 | tf_op jit(solution)/shard_map/all_to_all | solution.py:338
  170.2 12.8 %collective-permute-start.30 = (bf16[4,32,1024]{2,1,0:T(8,128)(2,1)}, bf16[4,32,1024]{2,1,0:T(8,128)(2,1)S(1)}, u32[]{:S(2)}, u32[]{:S(2)}) collective-permute-start(bf16[4,32,1024]{2,1,0:T(8,128)(2,1)} %copy-done.9), channel_id=1, source_target_pairs={{0,1},{1,0},{2,3},{3,2},{4,5},{5,4},{6,7},{7,6},{8,9},{9,8},{10,11... | collective-permute-start | bytes 786440 | tf_op jit(solution)/shard_map/ppermute | solution.py:264
  183.0 12.7 %collective-permute-start.33 = (bf16[64,1024]{1,0:T(8,128)(2,1)S(1)}, bf16[64,1024]{1,0:T(8,128)(2,1)S(1)}, u32[]{:S(2)}, u32[]{:S(2)}) collective-permute-start(bf16[64,1024]{1,0:T(8,128)(2,1)S(1)} %pad_maximum_fusion.4), channel_id=1, source_target_pairs={{0,6},{1,7},{2,0},{3,1},{4,2},{5,3},{6,4},{7,5},{8,14},{9,15},{10,... | collective-permute-start | bytes 393224 | tf_op jit(solution)/shard_map/ppermute | solution.py:264
  185.9 9.8 %collective-permute-start.32 = (bf16[64,1024]{1,0:T(8,128)(2,1)S(1)}, bf16[64,1024]{1,0:T(8,128)(2,1)S(1)}, u32[]{:S(2)}, u32[]{:S(2)}) collective-permute-start(bf16[64,1024]{1,0:T(8,128)(2,1)S(1)} %pad_maximum_fusion.3), channel_id=1, source_target_pairs={{0,4},{1,5},{2,6},{3,7},{4,0},{5,1},{6,2},{7,3},{8,12},{9,13},{10,... | collective-permute-start | bytes 393224 | tf_op jit(solution)/shard_map/ppermute | solution.py:264
  186.3 9.4 %collective-permute-start.31 = (bf16[64,1024]{1,0:T(8,128)(2,1)S(1)}, bf16[64,1024]{1,0:T(8,128)(2,1)S(1)}, u32[]{:S(2)}, u32[]{:S(2)}) collective-permute-start(bf16[64,1024]{1,0:T(8,128)(2,1)S(1)} %pad_maximum_fusion.2), channel_id=1, source_target_pairs={{0,2},{1,3},{2,4},{3,5},{4,6},{5,7},{6,0},{7,1},{8,10},{9,11},{10,... | collective-permute-start | bytes 393224 | tf_op jit(solution)/shard_map/ppermute | solution.py:264
  196.5 9.0 %all-to-all-start.1 = ((bf16[8,32,256]{2,1,0:T(8,128)(2,1)}), bf16[8,32,256]{2,1,0:T(8,128)(2,1)S(1)}, u32[]{:S(2)}, u32[]{:S(2)}) async-start(bf16[8,32,256]{2,1,0:T(8,128)(2,1)} %broadcast_in_dim.2), calls=%async_computation.1 | async-start | bytes 262144 | tf_op jit(solution)/shard_map/all_to_all | solution.py:303
  (16 other events, 54.3 us)
